TPU v7x, 32 devices: a whole 2x2x4 slice. The times are simulated.
32 devices in a mesh: sweep: 2 (over x), seq: 16 (over z, y, core).
Axes of the slice: x: 2, y: 2, z: 4, core: 2. Of those that a mesh axis runs over, the one named last changes fastest.
Arguments:
- queries: bfloat16 [6144, 4096], P(('sweep', 'seq')), parts along dimension 0, may hold values from -6 to 6
- keys: bfloat16 [6144, 4096], P(('sweep', 'seq')), parts along dimension 0, may hold values from -6 to 6
- values: bfloat16 [6144, 4096], P(('sweep', 'seq')), parts along dimension 0, may hold values from -6 to 6
- out_grad: bfloat16 [6144, 4096], P(('sweep', 'seq')), parts along dimension 0, may hold values from -6 to 6
- doc_blocks: int32 [8], P('sweep'), parts along dimension 0, may hold values from 1 to 10, 24 in all
Outputs:
- attn_out: bfloat16 [6144, 4096], P(('sweep', 'seq')), parts along dimension 0
- grad_q: bfloat16 [6144, 4096], P(('sweep', 'seq')), parts along dimension 0
- grad_k: bfloat16 [6144, 4096], P(('sweep', 'seq')), parts along dimension 0
- grad_v: bfloat16 [6144, 4096], P(('sweep', 'seq')), parts along dimension 0
There are 2 independent parts, one for each index of `sweep`. A program takes and returns all parts, laid end to end along the dimension named above; each array names one. Nothing has to cross between parts.
Inputs may be any that keep to these rules, and one draw needn't show every extreme that they name: `doc_blocks`: the lengths sum to 24 and the longest is exactly 10, so a document touches at most 8 consecutive blocks of 192 tokens.
All inputs are finite; a program needn't handle non-finite values.
Results may differ from a plain program's by a relative error of at most 0.012.
Values may be sent and summed in bfloat16 or wider, within the bound.
No kernel may reach another device: no remote copies, remote signals or barrier semaphores. Data moves between devices by JAX's collectives and lax.ppermute only.
A program may use at most 64 MiB of HBM per device.

v0:
```python
import math

import jax
import jax.numpy as jnp
from jax import lax
from jax.sharding import PartitionSpec as P

DH = 128
REACH = 8


def shifted(value, axis, by):
    devices = lax.axis_size(axis)
    pairs = [(i, i + by) for i in range(devices) if 0 <= i + by < devices]
    return lax.ppermute(value, axis, pairs)


def doc_number(spots_listing, doc_ends):
    counted = jnp.sum((spots_listing[:, None] >= doc_ends[None, :]).astype(jnp.int32), axis=1)
    return jnp.where(spots_listing < 0, jnp.int32(-1), counted)


def on_device(queries, keys, values, out_grad, doc_blocks):
    tok_rows = queries.shape[0]
    head_count = queries.shape[1] // DH
    longest = (REACH - 1) * tok_rows // 128
    out_scale = 1.0 / math.sqrt(DH * 32 * longest)
    first_pos = lax.axis_index("seq") * tok_rows
    doc_ends = jnp.cumsum(doc_blocks) * 128
    spots_listing = first_pos + lax.iota(jnp.int32, tok_rows)
    doc_ids = doc_number(spots_listing, doc_ends)
    edge_pos = jnp.stack([first_pos - 1, first_pos + tok_rows])
    edge_docs = doc_number(edge_pos, doc_ends)
    prev_doc = edge_docs[0]
    next_doc = edge_docs[1]
    query_per_head = queries.reshape(tok_rows, head_count, DH)
    key_per_head = keys.reshape(tok_rows, head_count, DH)
    value_per_head = values.reshape(tok_rows, head_count, DH)
    gradient_per_head = out_grad.reshape(tok_rows, head_count, DH)
    causal = lax.iota(jnp.int32, tok_rows)[:, None] >= lax.iota(jnp.int32, tok_rows)[None, :]
    allowed = (doc_ids[:, None] == doc_ids[None, :]) & causal
    tail_rows = doc_ids == doc_ids[tok_rows - 1]
    head_rows = doc_ids == doc_ids[0]
    zero_value = jnp.zeros((), queries.dtype)
    closing_memory = jnp.einsum(
        "oni,onw->niw",
        jnp.where(tail_rows[:, None, None], key_per_head, zero_value),
        value_per_head,
        preferred_element_type=jnp.float32,
    ).astype(jnp.bfloat16)
    channel_derivative = jnp.einsum(
        "oni,onw->niw",
        jnp.where(head_rows[:, None, None], query_per_head, zero_value),
        gradient_per_head,
        preferred_element_type=jnp.float32,
    ).astype(jnp.bfloat16)
    fwd_flag = (doc_ids[tok_rows - 1] != prev_doc).astype(jnp.bfloat16)
    bwd_flag = (doc_ids[0] != next_doc).astype(jnp.bfloat16)
    fwd_keep = 1.0 - fwd_flag.astype(jnp.float32)
    bwd_keep = 1.0 - bwd_flag.astype(jnp.float32)
    state_block = jnp.zeros((head_count, DH, DH), jnp.bfloat16)
    backward_block = jnp.zeros((head_count, DH, DH), jnp.bfloat16)
    for hop in range(REACH - 1):
        outgoing = (
            closing_memory.astype(jnp.float32) + fwd_keep * state_block.astype(jnp.float32)
        ).astype(jnp.bfloat16)
        state_block = shifted(outgoing, "seq", 1)
        returning = (
            channel_derivative.astype(jnp.float32) + bwd_keep * backward_block.astype(jnp.float32)
        ).astype(jnp.bfloat16)
        backward_block = shifted(returning, "seq", -1)
    input_selector = (doc_ids == prev_doc)[:, None, None]
    output_selector = (doc_ids == next_doc)[:, None, None]
    scores = jnp.einsum(
        "thd,shd->hts", query_per_head, key_per_head, preferred_element_type=jnp.float32
    )
    probs = jnp.where(allowed[None], scores, 0.0).astype(jnp.bfloat16)
    dscores = jnp.einsum(
        "thd,shd->hts", gradient_per_head, value_per_head, preferred_element_type=jnp.float32
    )
    dprobs = jnp.where(allowed[None], dscores, 0.0).astype(jnp.bfloat16)
    attention_core = jnp.einsum(
        "hts,shd->thd", probs, value_per_head, preferred_element_type=jnp.float32
    )
    attention_core = attention_core + jnp.where(
        input_selector,
        jnp.einsum("xra,ras->xrs", query_per_head, state_block, preferred_element_type=jnp.float32),
        0.0,
    )
    query_gradient = jnp.einsum(
        "hts,shd->thd", dprobs, key_per_head, preferred_element_type=jnp.float32
    )
    query_gradient = query_gradient + jnp.where(
        input_selector,
        jnp.einsum(
            "jox,odx->jod", gradient_per_head, state_block, preferred_element_type=jnp.float32
        ),
        0.0,
    )
    key_gradient = jnp.einsum(
        "hts,thd->shd", dprobs, query_per_head, preferred_element_type=jnp.float32
    )
    key_gradient = key_gradient + jnp.where(
        output_selector,
        jnp.einsum(
            "nom,ogm->nog", value_per_head, backward_block, preferred_element_type=jnp.float32
        ),
        0.0,
    )
    value_gradient = jnp.einsum(
        "hts,thd->shd", probs, gradient_per_head, preferred_element_type=jnp.float32
    )
    value_gradient = value_gradient + jnp.where(
        output_selector,
        jnp.einsum(
            "zlw,lwi->zli", key_per_head, backward_block, preferred_element_type=jnp.float32
        ),
        0.0,
    )
    width = head_count * DH
    attn_out = (out_scale * attention_core).astype(jnp.bfloat16).reshape(tok_rows, width)
    grad_q = (out_scale * query_gradient).astype(jnp.bfloat16).reshape(tok_rows, width)
    grad_k = (out_scale * key_gradient).astype(jnp.bfloat16).reshape(tok_rows, width)
    grad_v = (out_scale * value_gradient).astype(jnp.bfloat16).reshape(tok_rows, width)
    return (attn_out, grad_q, grad_k, grad_v)


def solution(mesh):
    return jax.shard_map(
        on_device,
        mesh=mesh,
        in_specs=(
            P(("sweep", "seq"), None),
            P(("sweep", "seq"), None),
            P(("sweep", "seq"), None),
            P(("sweep", "seq"), None),
            P("sweep"),
        ),
        out_specs=(
            P(("sweep", "seq"), None),
            P(("sweep", "seq"), None),
            P(("sweep", "seq"), None),
            P(("sweep", "seq"), None),
        ),
        check_vma=False,
    )
```

profile of v0, /device:TPU:1, one launch (start us, length us, event | category | flops | bytes accessed | tf_op | source)
XLA Modules:
  0.0 213.6 jit_solution(11240411614703895078)
XLA Ops:
  5.2 1.9 broadcast_compare_fusion
  7.1 3.9 %fusion.8 = (bf16[32,128,128]{2,1,0:T(8,128)(2,1)}, bf16[32,128,128]{2,1,0:T(8,128)(2,1)S(1)}) fusion(f32[]{:T(128)S(6)} %mul.95, pred[192]{0:T(512)(128)(4,1)S(1)} %get-tuple-element.7, bf16[192,4096]{1,0:T(8,128)(2,1)} %param.7, bf16[192,4096]{1,0:T(8,128)(2,1)} %param.6), kind=kOutput, calls=%fused_computation.28 | convolution fusion | flops 204210176 | bytes 5243076 | tf_op jit(solution)/shard_map/oni,onw->niw/dot_general | solution.py:45
  11.0 4.5 %collective-permute-start = (bf16[32,128,128]{2,1,0:T(8,128)(2,1)}, bf16[32,128,128]{2,1,0:T(8,128)(2,1)}, u32[]{:S(2)}, u32[]{:S(2)}) collective-permute-start(bf16[32,128,128]{2,1,0:T(8,128)(2,1)} %get-tuple-element.13), channel_id=1, source_target_pairs={{0,1},{1,2},{2,3},{3,4},{4,5},{5,6},{6,7},{7,8},{8,9},{9,10},{10,1... | collective-permute-start | bytes 3145736 | tf_op jit(solution)/shard_map/ppermute | solution.py:15
  16.9 2.5 %fusion.15 = (bf16[32,128,128]{2,1,0:T(8,128)(2,1)S(1)}, bf16[32,128,128]{2,1,0:T(8,128)(2,1)S(1)}) fusion(f32[]{:T(128)S(6)} %mul.106, pred[192]{0:T(512)(128)(4,1)S(1)} %get-tuple-element.6, bf16[192,4096]{1,0:T(8,128)(2,1)} %param.8, bf16[192,4096]{1,0:T(8,128)(2,1)S(1)} %copy-done), kind=kOutput, calls=%fused_computation.35 | convolution fusion | flops 204210176 | bytes 5243076 | tf_op jit(solution)/shard_map/oni,onw->niw/dot_general | solution.py:51
  19.3 1.9 collective-permute-start.7
  21.3 17.5 %collective-permute-done = bf16[32,128,128]{2,1,0:T(8,128)(2,1)} collective-permute-done((bf16[32,128,128]{2,1,0:T(8,128)(2,1)}, bf16[32,128,128]{2,1,0:T(8,128)(2,1)}, u32[]{:S(2)}, u32[]{:S(2)}) %collective-permute-start) | collective-permute-done | bytes 1048608 | tf_op jit(solution)/shard_map/ppermute | solution.py:15
  38.8 1.6 fusion.9
  40.4 4.4 %collective-permute-start.1 = (bf16[32,128,128]{2,1,0:T(8,128)(2,1)S(1)}, bf16[32,128,128]{2,1,0:T(8,128)(2,1)S(1)}, u32[]{:S(2)}, u32[]{:S(2)}) collective-permute-start(bf16[32,128,128]{2,1,0:T(8,128)(2,1)S(1)} %fusion.9), channel_id=1, source_target_pairs={{0,1},{1,2},{2,3},{3,4},{4,5},{5,6},{6,7},{7,8},{8,9},{9,10},{10,1... | collective-permute-start | bytes 3145736 | tf_op jit(solution)/shard_map/ppermute | solution.py:15
  45.3 1.9 collective-permute-start.8
  47.2 20.5 %collective-permute-done.1 = bf16[32,128,128]{2,1,0:T(8,128)(2,1)S(1)} collective-permute-done((bf16[32,128,128]{2,1,0:T(8,128)(2,1)S(1)}, bf16[32,128,128]{2,1,0:T(8,128)(2,1)S(1)}, u32[]{:S(2)}, u32[]{:S(2)}) %collective-permute-start.1) | collective-permute-done | bytes 1048608 | tf_op jit(solution)/shard_map/ppermute | solution.py:15
  68.2 4.4 %collective-permute-start.2 = (bf16[32,128,128]{2,1,0:T(8,128)(2,1)S(1)}, bf16[32,128,128]{2,1,0:T(8,128)(2,1)S(1)}, u32[]{:S(2)}, u32[]{:S(2)}) collective-permute-start(bf16[32,128,128]{2,1,0:T(8,128)(2,1)S(1)} %fusion.10), channel_id=1, source_target_pairs={{0,1},{1,2},{2,3},{3,4},{4,5},{5,6},{6,7},{7,8},{8,9},{9,10},{10,1... | collective-permute-start | bytes 3145736 | tf_op jit(solution)/shard_map/ppermute | solution.py:15
  73.0 1.9 collective-permute-start.9
  75.0 20.5 %collective-permute-done.2 = bf16[32,128,128]{2,1,0:T(8,128)(2,1)S(1)} collective-permute-done((bf16[32,128,128]{2,1,0:T(8,128)(2,1)S(1)}, bf16[32,128,128]{2,1,0:T(8,128)(2,1)S(1)}, u32[]{:S(2)}, u32[]{:S(2)}) %collective-permute-start.2) | collective-permute-done | bytes 1048608 | tf_op jit(solution)/shard_map/ppermute | solution.py:15
  95.9 4.4 %collective-permute-start.3 = (bf16[32,128,128]{2,1,0:T(8,128)(2,1)S(1)}, bf16[32,128,128]{2,1,0:T(8,128)(2,1)S(1)}, u32[]{:S(2)}, u32[]{:S(2)}) collective-permute-start(bf16[32,128,128]{2,1,0:T(8,128)(2,1)S(1)} %fusion.11), channel_id=1, source_target_pairs={{0,1},{1,2},{2,3},{3,4},{4,5},{5,6},{6,7},{7,8},{8,9},{9,10},{10,1... | collective-permute-start | bytes 3145736 | tf_op jit(solution)/shard_map/ppermute | solution.py:15
  100.9 2.1 collective-permute-start.10
  103.0 20.3 %collective-permute-done.3 = bf16[32,128,128]{2,1,0:T(8,128)(2,1)S(1)} collective-permute-done((bf16[32,128,128]{2,1,0:T(8,128)(2,1)S(1)}, bf16[32,128,128]{2,1,0:T(8,128)(2,1)S(1)}, u32[]{:S(2)}, u32[]{:S(2)}) %collective-permute-start.3) | collective-permute-done | bytes 1048608 | tf_op jit(solution)/shard_map/ppermute | solution.py:15
  123.7 4.5 %collective-permute-start.4 = (bf16[32,128,128]{2,1,0:T(8,128)(2,1)S(1)}, bf16[32,128,128]{2,1,0:T(8,128)(2,1)S(1)}, u32[]{:S(2)}, u32[]{:S(2)}) collective-permute-start(bf16[32,128,128]{2,1,0:T(8,128)(2,1)S(1)} %fusion.12), channel_id=1, source_target_pairs={{0,1},{1,2},{2,3},{3,4},{4,5},{5,6},{6,7},{7,8},{8,9},{9,10},{10,1... | collective-permute-start | bytes 3145736 | tf_op jit(solution)/shard_map/ppermute | solution.py:15
  128.2 1.1 select_convert_fusion.1
  129.3 1.3 fusion.22
  131.1 2.1 collective-permute-start.11
  133.2 18.0 %collective-permute-done.4 = bf16[32,128,128]{2,1,0:T(8,128)(2,1)S(1)} collective-permute-done((bf16[32,128,128]{2,1,0:T(8,128)(2,1)S(1)}, bf16[32,128,128]{2,1,0:T(8,128)(2,1)S(1)}, u32[]{:S(2)}, u32[]{:S(2)}) %collective-permute-start.4) | collective-permute-done | bytes 1048608 | tf_op jit(solution)/shard_map/ppermute | solution.py:15
  151.5 4.6 %collective-permute-start.5 = (bf16[32,128,128]{2,1,0:T(8,128)(2,1)S(1)}, bf16[32,128,128]{2,1,0:T(8,128)(2,1)S(1)}, u32[]{:S(2)}, u32[]{:S(2)}) collective-permute-start(bf16[32,128,128]{2,1,0:T(8,128)(2,1)S(1)} %fusion.13), channel_id=1, source_target_pairs={{0,1},{1,2},{2,3},{3,4},{4,5},{5,6},{6,7},{7,8},{8,9},{9,10},{10,1... | collective-permute-start | bytes 3145736 | tf_op jit(solution)/shard_map/ppermute | solution.py:15
  156.1 1.0 select_convert_fusion
  158.6 1.9 collective-permute-start.12
  160.5 18.4 %collective-permute-done.5 = bf16[32,128,128]{2,1,0:T(8,128)(2,1)S(1)} collective-permute-done((bf16[32,128,128]{2,1,0:T(8,128)(2,1)S(1)}, bf16[32,128,128]{2,1,0:T(8,128)(2,1)S(1)}, u32[]{:S(2)}, u32[]{:S(2)}) %collective-permute-start.5) | collective-permute-done | bytes 1048608 | tf_op jit(solution)/shard_map/ppermute | solution.py:15
  179.3 4.4 %collective-permute-start.6 = (bf16[32,128,128]{2,1,0:T(8,128)(2,1)S(1)}, bf16[32,128,128]{2,1,0:T(8,128)(2,1)S(1)}, u32[]{:S(2)}, u32[]{:S(2)}) collective-permute-start(bf16[32,128,128]{2,1,0:T(8,128)(2,1)S(1)} %fusion.14), channel_id=1, source_target_pairs={{0,1},{1,2},{2,3},{3,4},{4,5},{5,6},{6,7},{7,8},{8,9},{9,10},{10,1... | collective-permute-start | bytes 3145736 | tf_op jit(solution)/shard_map/ppermute | solution.py:15
  183.7 1.3 fusion.38
  185.0 1.0 fusion.35
  186.5 1.9 collective-permute-start.13
  188.4 17.7 %collective-permute-done.6 = bf16[32,128,128]{2,1,0:T(8,128)(2,1)S(1)} collective-permute-done((bf16[32,128,128]{2,1,0:T(8,128)(2,1)S(1)}, bf16[32,128,128]{2,1,0:T(8,128)(2,1)S(1)}, u32[]{:S(2)}, u32[]{:S(2)}) %collective-permute-start.6) | collective-permute-done | bytes 1048608 | tf_op jit(solution)/shard_map/ppermute | solution.py:15
  207.7 2.1 copy_bitcast_fusion.2
  211.5 2.1 %copy_bitcast_fusion = (bf16[192,4096]{1,0:T(8,128)(2,1)}, bf16[192,4096]{1,0:T(8,128)(2,1)}) fusion(bf16[32,24,8,128]{3,2,1,0:T(8,128)(2,1)S(1)} %fusion.53, bf16[32,24,8,128]{3,2,1,0:T(8,128)(2,1)S(1)} %fusion.50), kind=kLoop, calls=%fused_computation.42 | loop fusion | bytes 6291456 | tf_op jit(solution)/shard_map/reshape | solution.py:124
  (42 shorter events, 12.2 us)
Async XLA Ops:
  0.6 16.2 %copy-start = (bf16[192,4096]{1,0:T(8,128)(2,1)S(1)}, bf16[192,4096]{1,0:T(8,128)(2,1)}, u32[]{:S(2)}) copy-start(bf16[192,4096]{1,0:T(8,128)(2,1)} %param.5) | copy-start | bytes 4718596
  11.0 27.8 %collective-permute-start = (bf16[32,128,128]{2,1,0:T(8,128)(2,1)}, bf16[32,128,128]{2,1,0:T(8,128)(2,1)}, u32[]{:S(2)}, u32[]{:S(2)}) collective-permute-start(bf16[32,128,128]{2,1,0:T(8,128)(2,1)} %get-tuple-element.13), channel_id=1, source_target_pairs={{0,1},{1,2},{2,3},{3,4},{4,5},{5,6},{6,7},{7,8},{8,9},{9,10},{10,1... | collective-permute-start | bytes 3145736 | tf_op jit(solution)/shard_map/ppermute | solution.py:15
  19.3 25.5 %collective-permute-start.7 = (bf16[32,128,128]{2,1,0:T(8,128)(2,1)S(1)}, bf16[32,128,128]{2,1,0:T(8,128)(2,1)S(1)}, u32[]{:S(2)}, u32[]{:S(2)}) collective-permute-start(bf16[32,128,128]{2,1,0:T(8,128)(2,1)S(1)} %get-tuple-element.15), channel_id=1, source_target_pairs={{1,0},{2,1},{3,2},{4,3},{5,4},{6,5},{7,6},{8,7},{9,8},{10,9},{11,1... | collective-permute-start | bytes 3145736 | tf_op jit(solution)/shard_map/ppermute | solution.py:15
  40.4 27.4 %collective-permute-start.1 = (bf16[32,128,128]{2,1,0:T(8,128)(2,1)S(1)}, bf16[32,128,128]{2,1,0:T(8,128)(2,1)S(1)}, u32[]{:S(2)}, u32[]{:S(2)}) collective-permute-start(bf16[32,128,128]{2,1,0:T(8,128)(2,1)S(1)} %fusion.9), channel_id=1, source_target_pairs={{0,1},{1,2},{2,3},{3,4},{4,5},{5,6},{6,7},{7,8},{8,9},{9,10},{10,1... | collective-permute-start | bytes 3145736 | tf_op jit(solution)/shard_map/ppermute | solution.py:15
  45.3 27.3 %collective-permute-start.8 = (bf16[32,128,128]{2,1,0:T(8,128)(2,1)S(1)}, bf16[32,128,128]{2,1,0:T(8,128)(2,1)S(1)}, u32[]{:S(2)}, u32[]{:S(2)}) collective-permute-start(bf16[32,128,128]{2,1,0:T(8,128)(2,1)S(1)} %fusion.16), channel_id=1, source_target_pairs={{1,0},{2,1},{3,2},{4,3},{5,4},{6,5},{7,6},{8,7},{9,8},{10,9},{11,1... | collective-permute-start | bytes 3145736 | tf_op jit(solution)/shard_map/ppermute | solution.py:15
  68.2 27.4 %collective-permute-start.2 = (bf16[32,128,128]{2,1,0:T(8,128)(2,1)S(1)}, bf16[32,128,128]{2,1,0:T(8,128)(2,1)S(1)}, u32[]{:S(2)}, u32[]{:S(2)}) collective-permute-start(bf16[32,128,128]{2,1,0:T(8,128)(2,1)S(1)} %fusion.10), channel_id=1, source_target_pairs={{0,1},{1,2},{2,3},{3,4},{4,5},{5,6},{6,7},{7,8},{8,9},{9,10},{10,1... | collective-permute-start | bytes 3145736 | tf_op jit(solution)/shard_map/ppermute | solution.py:15
  73.0 27.4 %collective-permute-start.9 = (bf16[32,128,128]{2,1,0:T(8,128)(2,1)S(1)}, bf16[32,128,128]{2,1,0:T(8,128)(2,1)S(1)}, u32[]{:S(2)}, u32[]{:S(2)}) collective-permute-start(bf16[32,128,128]{2,1,0:T(8,128)(2,1)S(1)} %fusion.17), channel_id=1, source_target_pairs={{1,0},{2,1},{3,2},{4,3},{5,4},{6,5},{7,6},{8,7},{9,8},{10,9},{11,1... | collective-permute-start | bytes 3145736 | tf_op jit(solution)/shard_map/ppermute | solution.py:15
  95.9 27.4 %collective-permute-start.3 = (bf16[32,128,128]{2,1,0:T(8,128)(2,1)S(1)}, bf16[32,128,128]{2,1,0:T(8,128)(2,1)S(1)}, u32[]{:S(2)}, u32[]{:S(2)}) collective-permute-start(bf16[32,128,128]{2,1,0:T(8,128)(2,1)S(1)} %fusion.11), channel_id=1, source_target_pairs={{0,1},{1,2},{2,3},{3,4},{4,5},{5,6},{6,7},{7,8},{8,9},{9,10},{10,1... | collective-permute-start | bytes 3145736 | tf_op jit(solution)/shard_map/ppermute | solution.py:15
  100.9 27.3 %copy-start.2 = (bf16[192,4096]{1,0:T(8,128)(2,1)S(1)}, bf16[192,4096]{1,0:T(8,128)(2,1)}, u32[]{:S(2)}) copy-start(bf16[192,4096]{1,0:T(8,128)(2,1)} %param.6) | copy-start | bytes 4718596
  100.9 29.7 %collective-permute-start.10 = (bf16[32,128,128]{2,1,0:T(8,128)(2,1)S(1)}, bf16[32,128,128]{2,1,0:T(8,128)(2,1)S(1)}, u32[]{:S(2)}, u32[]{:S(2)}) collective-permute-start(bf16[32,128,128]{2,1,0:T(8,128)(2,1)S(1)} %fusion.18), channel_id=1, source_target_pairs={{1,0},{2,1},{3,2},{4,3},{5,4},{6,5},{7,6},{8,7},{9,8},{10,9},{11,1... | collective-permute-start | bytes 3145736 | tf_op jit(solution)/shard_map/ppermute | solution.py:15
  123.7 5.6 %copy-start.1 = (bf16[192,4096]{1,0:T(8,128)(2,1)S(1)}, bf16[192,4096]{1,0:T(8,128)(2,1)}, u32[]{:S(2)}) copy-start(bf16[192,4096]{1,0:T(8,128)(2,1)} %param.8) | copy-start | bytes 4718596
  123.7 27.5 %collective-permute-start.4 = (bf16[32,128,128]{2,1,0:T(8,128)(2,1)S(1)}, bf16[32,128,128]{2,1,0:T(8,128)(2,1)S(1)}, u32[]{:S(2)}, u32[]{:S(2)}) collective-permute-start(bf16[32,128,128]{2,1,0:T(8,128)(2,1)S(1)} %fusion.12), channel_id=1, source_target_pairs={{0,1},{1,2},{2,3},{3,4},{4,5},{5,6},{6,7},{7,8},{8,9},{9,10},{10,1... | collective-permute-start | bytes 3145736 | tf_op jit(solution)/shard_map/ppermute | solution.py:15
  131.1 25.0 %copy-start.3 = (bf16[192,4096]{1,0:T(8,128)(2,1)S(1)}, bf16[192,4096]{1,0:T(8,128)(2,1)}, u32[]{:S(2)}) copy-start(bf16[192,4096]{1,0:T(8,128)(2,1)} %param.7) | copy-start | bytes 4718596
  131.1 27.0 %collective-permute-start.11 = (bf16[32,128,128]{2,1,0:T(8,128)(2,1)S(1)}, bf16[32,128,128]{2,1,0:T(8,128)(2,1)S(1)}, u32[]{:S(2)}, u32[]{:S(2)}) collective-permute-start(bf16[32,128,128]{2,1,0:T(8,128)(2,1)S(1)} %fusion.19), channel_id=1, source_target_pairs={{1,0},{2,1},{3,2},{4,3},{5,4},{6,5},{7,6},{8,7},{9,8},{10,9},{11,1... | collective-permute-start | bytes 3145736 | tf_op jit(solution)/shard_map/ppermute | solution.py:15
  151.5 27.4 %collective-permute-start.5 = (bf16[32,128,128]{2,1,0:T(8,128)(2,1)S(1)}, bf16[32,128,128]{2,1,0:T(8,128)(2,1)S(1)}, u32[]{:S(2)}, u32[]{:S(2)}) collective-permute-start(bf16[32,128,128]{2,1,0:T(8,128)(2,1)S(1)} %fusion.13), channel_id=1, source_target_pairs={{0,1},{1,2},{2,3},{3,4},{4,5},{5,6},{6,7},{7,8},{8,9},{9,10},{10,1... | collective-permute-start | bytes 3145736 | tf_op jit(solution)/shard_map/ppermute | solution.py:15
  158.6 27.4 %collective-permute-start.12 = (bf16[32,128,128]{2,1,0:T(8,128)(2,1)S(1)}, bf16[32,128,128]{2,1,0:T(8,128)(2,1)S(1)}, u32[]{:S(2)}, u32[]{:S(2)}) collective-permute-start(bf16[32,128,128]{2,1,0:T(8,128)(2,1)S(1)} %fusion.20), channel_id=1, source_target_pairs={{1,0},{2,1},{3,2},{4,3},{5,4},{6,5},{7,6},{8,7},{9,8},{10,9},{11,1... | collective-permute-start | bytes 3145736 | tf_op jit(solution)/shard_map/ppermute | solution.py:15
  179.3 26.8 %collective-permute-start.6 = (bf16[32,128,128]{2,1,0:T(8,128)(2,1)S(1)}, bf16[32,128,128]{2,1,0:T(8,128)(2,1)S(1)}, u32[]{:S(2)}, u32[]{:S(2)}) collective-permute-start(bf16[32,128,128]{2,1,0:T(8,128)(2,1)S(1)} %fusion.14), channel_id=1, source_target_pairs={{0,1},{1,2},{2,3},{3,4},{4,5},{5,6},{6,7},{7,8},{8,9},{9,10},{10,1... | collective-permute-start | bytes 3145736 | tf_op jit(solution)/shard_map/ppermute | solution.py:15
  186.5 23.4 %collective-permute-start.13 = (bf16[32,128,128]{2,1,0:T(8,128)(2,1)S(1)}, bf16[32,128,128]{2,1,0:T(8,128)(2,1)S(1)}, u32[]{:S(2)}, u32[]{:S(2)}) collective-permute-start(bf16[32,128,128]{2,1,0:T(8,128)(2,1)S(1)} %fusion.21), channel_id=1, source_target_pairs={{1,0},{2,1},{3,2},{4,3},{5,4},{6,5},{7,6},{8,7},{9,8},{10,9},{11,1... | collective-permute-start | bytes 3145736 | tf_op jit(solution)/shard_map/ppermute | solution.py:15
where the time goes:
time: 214 us
  waiting for transfers between devices  133 us (62%)
  starting transfers between devices  44.9 us (21%)
  matrix products  16.2 us (8%)
  other arithmetic  10.3 us (5%)
  local copies, waits for them, and re-layouts  5.47 us (3%)
  between operations  3.68 us (2%)
    ppermute x14, waiting for transfers between devices, shifted(): return lax.ppermute(value, axis, pairs)  133 us
    ppermute x14, starting transfers between devices, shifted(): return lax.ppermute(value, axis, pairs)  44.9 us
  transfers between devices with their start and end apart: 14, of which 7 were waited for; matrix products, arithmetic and copies ran while one was open for 9% of the time, Pallas kernels for 0%

commit v1 on v0

v1 whole, which is shorter than its diff:
```python
import functools
import math

import jax
import jax.numpy as jnp
from jax import lax
from jax.experimental import pallas as pl
from jax.experimental.pallas import tpu as pltpu
from jax.sharding import PartitionSpec as P

DH = 128
UNIT = 128
LONGEST = 10
F32 = jnp.float32
BF16 = jnp.bfloat16


def doc_of(pos, doc_ref, docs):
    count = jnp.int32(0)
    end = jnp.int32(0)
    for d in range(docs):
        end = end + doc_ref[d] * UNIT
        count = count + (pos >= end).astype(jnp.int32)
    return jnp.where(pos < 0, jnp.int32(-1), count)


def edges(pos_ref, doc_ref, rows, docs):
    first = pos_ref[0] * rows
    start = jnp.int32(0)
    stop = jnp.int32(1 << 30)
    end = jnp.int32(0)
    for d in range(docs):
        end = end + doc_ref[d] * UNIT
        start = jnp.where(end <= first + (rows - 1), end, start)
        stop = jnp.minimum(stop, jnp.where(end > first, end, jnp.int32(1 << 30)))
    return start - first, stop - first


def dot_tt(a, b):
    return lax.dot_general(a, b, (((0,), (0,)), ((), ())), preferred_element_type=F32)


def dot_nt(a, b):
    return lax.dot_general(a, b, (((1,), (1,)), ((), ())), preferred_element_type=F32)


def dot_nn(a, b):
    return lax.dot_general(a, b, (((1,), (0,)), ((), ())), preferred_element_type=F32)


def tails_kernel(pos_ref, doc_ref, q_ref, k_ref, v_ref, g_ref, keep_ref, send_ref, w_ref, *, docs, heads):
    rows = q_ref.shape[0]
    dev = pos_ref[0]
    core = lax.rem(dev, 2)
    start, stop = edges(pos_ref, doc_ref, rows, docs)
    row = lax.broadcasted_iota(jnp.int32, (rows, DH), 0)
    in_tail = row >= start
    in_head = row < stop

    @pl.when(pl.program_id(0) == 0)
    def _():
        chip = dev - core

        def key(u):
            pos = jnp.where(core == 0, rows * (chip + 2 - u) - 1, rows * (chip + u))
            return doc_of(pos, doc_ref, docs)

        k0, k1, k2, k4 = key(0), key(1), key(2), key(4)
        same = (k1 == k0, k2 == k0, k4 == k2, k4 == k0, k2 == k1)
        for i, flag in enumerate(same):
            w_ref[i] = flag.astype(F32)
        for i in range(len(same), 8):
            w_ref[i] = jnp.float32(0)

    zero = jnp.zeros((), BF16)
    for i in range(heads):
        cols = pl.ds(i * DH, DH)
        tail = dot_tt(jnp.where(in_tail, k_ref[:, cols], zero), v_ref[:, cols]).astype(BF16)
        head = dot_tt(jnp.where(in_head, q_ref[:, cols], zero), g_ref[:, cols]).astype(BF16)
        keep_ref[i] = jnp.where(core == 0, tail, head)
        send_ref[i] = jnp.where(core == 0, head, tail)


def local_kernel(pos_ref, doc_ref, q_ref, k_ref, v_ref, g_ref, o_ref, dq_ref, dk_ref, dv_ref, mask_ref, *, docs, heads, scale):
    rows = q_ref.shape[0]

    @pl.when(pl.program_id(0) == 0)
    def _():
        start, _ = edges(pos_ref, doc_ref, rows, docs)
        t = lax.broadcasted_iota(jnp.int32, (rows, rows), 0)
        s = lax.broadcasted_iota(jnp.int32, (rows, rows), 1)
        allowed = (s <= t) & ((t < start) | (s >= start))
        mask_ref[...] = allowed.astype(F32)

    allowed = mask_ref[...] > 0
    for i in range(heads):
        cols = pl.ds(i * DH, DH)
        q, k, v, g = q_ref[:, cols], k_ref[:, cols], v_ref[:, cols], g_ref[:, cols]
        probs = jnp.where(allowed, dot_nt(q, k), 0.0).astype(BF16)
        dprobs = jnp.where(allowed, dot_nt(g, v), 0.0).astype(BF16)
        o_ref[:, cols] = (scale * dot_nn(probs, v)).astype(BF16)
        dq_ref[:, cols] = (scale * dot_nn(dprobs, k)).astype(BF16)
        dk_ref[:, cols] = (scale * dot_tt(dprobs, q)).astype(BF16)
        dv_ref[:, cols] = (scale * dot_tt(probs, g)).astype(BF16)


def final_kernel(pos_ref, doc_ref, q_ref, k_ref, v_ref, g_ref, mine_ref, other_ref, o_in, dq_in, dk_in, dv_in, o_ref, dq_ref, dk_ref, dv_ref, *, docs, heads, scale):
    rows = q_ref.shape[0]
    dev = pos_ref[0]
    forward = lax.rem(dev, 2) == 0
    first = dev * rows
    prev_doc = doc_of(first - 1, doc_ref, docs)
    next_doc = doc_of(first + rows, doc_ref, docs)
    first_doc = doc_of(first, doc_ref, docs)
    last_doc = doc_of(first + (rows - 1), doc_ref, docs)
    start, stop = edges(pos_ref, doc_ref, rows, docs)
    row = lax.broadcasted_iota(jnp.int32, (rows, DH), 0)
    into = jnp.where(first_doc == prev_doc, stop, 0)
    onto = jnp.where(last_doc == next_doc, start, rows)
    reads = row < into
    feeds = row >= onto
    for i in range(heads):
        cols = pl.ds(i * DH, DH)
        q, k, v, g = q_ref[:, cols], k_ref[:, cols], v_ref[:, cols], g_ref[:, cols]
        state = jnp.where(forward, mine_ref[i], other_ref[i])
        back = jnp.where(forward, other_ref[i], mine_ref[i])
        o_ref[:, cols] = (o_in[:, cols].astype(F32) + jnp.where(reads, scale * dot_nn(q, state), 0.0)).astype(BF16)
        dq_ref[:, cols] = (dq_in[:, cols].astype(F32) + jnp.where(reads, scale * dot_nt(g, state), 0.0)).astype(BF16)
        dk_ref[:, cols] = (dk_in[:, cols].astype(F32) + jnp.where(feeds, scale * dot_nt(v, back), 0.0)).astype(BF16)
        dv_ref[:, cols] = (dv_in[:, cols].astype(F32) + jnp.where(feeds, scale * dot_nn(k, back), 0.0)).astype(BF16)


def on_device(queries, keys, values, out_grad, doc_blocks):
    rows, width = queries.shape
    n_heads = width // DH
    docs = doc_blocks.shape[0]
    devices = lax.axis_size("seq")
    scale = 1.0 / math.sqrt(DH * n_heads * LONGEST)
    dev = lax.axis_index("seq").astype(jnp.int32).reshape(1)
    args = (queries, keys, values, out_grad)
    smem = pl.BlockSpec(memory_space=pltpu.SMEM)
    params = pltpu.CompilerParams(dimension_semantics=("arbitrary",))
    hb = 2

    def wide(off):
        return pl.BlockSpec((rows, hb * DH), lambda i: (0, i + off // hb))

    square = pl.BlockSpec((hb, DH, DH), lambda i: (i, 0, 0))

    def tails(lo, n):
        return pl.pallas_call(
            functools.partial(tails_kernel, docs=docs, heads=hb),
            grid=(n // hb,),
            in_specs=[smem, smem] + [wide(lo)] * 4,
            out_specs=[square, square, smem],
            out_shape=[jax.ShapeDtypeStruct((n, DH, DH), BF16)] * 2 + [jax.ShapeDtypeStruct((8,), F32)],
            compiler_params=params,
            cost_estimate=pl.CostEstimate(flops=4 * n * rows * DH * DH, transcendentals=0, bytes_accessed=n * DH * (8 * rows + 4 * DH)),
            name="tails",
        )(dev, doc_blocks, *args)

    def local(lo, n):
        return pl.pallas_call(
            functools.partial(local_kernel, docs=docs, heads=hb, scale=scale),
            grid=(n // hb,),
            in_specs=[smem, smem] + [wide(lo)] * 4,
            out_specs=[wide(0)] * 4,
            out_shape=[jax.ShapeDtypeStruct((rows, n * DH), BF16)] * 4,
            scratch_shapes=[pltpu.VMEM((rows, rows), F32)],
            compiler_params=params,
            cost_estimate=pl.CostEstimate(flops=12 * n * rows * rows * DH, transcendentals=0, bytes_accessed=16 * n * DH * rows),
            name="local",
        )(dev, doc_blocks, *args)

    def final(lo, n, mine, other, partial, outs):
        aliased = [] if outs is None else list(outs)
        keep = [pl.BlockSpec(memory_space=pl.ANY)] * len(aliased)
        body = functools.partial(final_kernel, docs=docs, heads=hb, scale=scale)
        if aliased:
            inner = body

            def body(*refs):
                inner(*refs[:12], *refs[16:])

        return pl.pallas_call(
            body,
            grid=(n // hb,),
            in_specs=[smem, smem] + [wide(lo)] * 4 + [square] * 2 + [wide(0)] * 4 + keep,
            out_specs=[wide(lo)] * 4,
            out_shape=[jax.ShapeDtypeStruct((rows, width), BF16)] * 4,
            input_output_aliases={12 + i: i for i in range(len(aliased))},
            compiler_params=params,
            cost_estimate=pl.CostEstimate(flops=8 * n * rows * DH * DH, transcendentals=0, bytes_accessed=24 * n * DH * rows),
            name="final",
        )(dev, doc_blocks, *args, mine, other, *partial, *aliased)

    def across(x):
        return lax.ppermute(x, "seq", [(i, i ^ 1) for i in range(devices)])

    def along(x, by):
        pairs = [(i, i + by if i % 2 == 0 else i - by) for i in range(devices)]
        return lax.ppermute(x, "seq", [(i, j) for i, j in pairs if 0 <= j < devices])

    def fma(base, w, x):
        return (base.astype(F32) + w * x.astype(F32)).astype(BF16)

    n_x = 18
    sizes = ((0, n_x), (n_x, n_heads - n_x))
    keep_x, send_x, w = tails(*sizes[0])
    keep_w, send_w, _ = tails(*sizes[1])
    total_x = fma(across(send_x), w[0], keep_x)
    total_w = fma(across(send_w), w[0], keep_w)
    part_x = local(*sizes[0])
    part_w = local(*sizes[1])
    near_x = along(total_x, 2)
    far_w = along(total_w, 4)
    gathered_w = fma(total_w, w[3], far_w)
    near_w = along(gathered_w, 2)
    near_x, _ = lax.optimization_barrier((near_x, gathered_w))
    gathered_x = fma(total_x, w[1], near_x)
    far_x = along(gathered_x, 4)
    mine_x = fma(near_x, w[2], far_x)
    mine_w = fma(near_w, w[2], far_w)
    other_x = across(fma(keep_x, w[4], mine_x))
    other_w = across(fma(keep_w, w[4], mine_w))
    outs = final(*sizes[0], mine_x, other_x, part_x, None)
    outs = final(*sizes[1], mine_w, other_w, part_w, outs)
    return tuple(outs)


def solution(mesh):
    spec = P(("sweep", "seq"), None)
    return jax.shard_map(
        on_device,
        mesh=mesh,
        in_specs=(spec, spec, spec, spec, P("sweep")),
        out_specs=(spec, spec, spec, spec),
        check_vma=False,
    )
```

time: 214 us -> 101 us (0.47)
  the two profiles are of different devices: /device:TPU:1 before, /device:TPU:15 now
where the time goes in v1:
time: 101 us; the launch traced here: 99.2 us
  Pallas kernels  49.6 us (49%)
  starting transfers between devices  20.2 us (20%)
  waiting for transfers between devices  17.5 us (17%)
  other arithmetic  8.04 us (8%)
  local copies, waits for them, and re-layouts  3.08 us (3%)
    pallas_call x2, Pallas kernels, local(): pl.pallas_call(functools.partial(local_kernel, docs=docs, heads=hb, scale...  18.9 us
    ppermute x4, waiting for transfers between devices, along(): lax.ppermute(x, 'seq', [(i, j) for i, j in pairs if 0 <= j < devices])  17.5 us
    pallas_call x2, Pallas kernels, final(): pl.pallas_call(body, grid=(n // hb,), in_specs=[smem, smem] + [wide(lo)]...  16.6 us
    pallas_call x2, Pallas kernels, tails(): pl.pallas_call(functools.partial(tails_kernel, docs=docs, heads=hb), grid...  14 us
    ppermute x4, starting transfers between devices, across(): return lax.ppermute(x, 'seq', [(i, i ^ 1) for i in range(devices)])  10.3 us
    ppermute x4, starting transfers between devices, along(): lax.ppermute(x, 'seq', [(i, j) for i, j in pairs if 0 <= j < devices])  9.95 us
    convert_element_type x6, other arithmetic, fma(): return (base.astype(F32) + w * x.astype(F32)).astype(BF16)  8.04 us
  transfers between devices with their start and end apart: 8, of which 3 were waited for; matrix products, arithmetic and copies ran while one was open for 9% of the time, Pallas kernels for 36%

profile of v1, /device:TPU:15, one launch (start us, length us, event | category | flops | bytes accessed | tf_op | source)
XLA Modules:
  0.0 99.2 jit_solution(11616621358225788422)
XLA Ops:
  0.6 6.3 %tails.2 = (bf16[14,128,128]{2,1,0:T(8,128)(2,1)}, bf16[14,128,128]{2,1,0:T(8,128)(2,1)}, f32[8]{0:T(128)}) custom-call(s32[1]{0:T(128)} %bitcast.pos_ref.refs_0_, s32[4]{0:T(128)} %refs_1_.1, bf16[192,4096]{1,0:T(8,128)(2,1)} %refs_2_.1, bf16[192,4096]{1,0:T(8,128)(2,1)} %refs_3_.1, bf16[192,4096]{1,0:T(8,128)(2,1)} %refs_4_.1, bf16[192,4096]{1,0:T(8,128)(2,1)} %refs_5_.1), custom_call_target="tpu_custom_call" | custom-call | flops 176160768 | bytes 3670016 | tf_op jit(solution)/shard_map/tails/pallas_call | solution.py:151
  6.9 0.7 collective-permute-start
  7.7 7.7 %tails.3 = (bf16[18,128,128]{2,1,0:T(8,128)(2,1)}, bf16[18,128,128]{2,1,0:T(8,128)(2,1)}, f32[8]{0:T(128)}) custom-call(s32[1]{0:T(128)} %bitcast.pos_ref.refs_0_, s32[4]{0:T(128)} %refs_1_.1, bf16[192,4096]{1,0:T(8,128)(2,1)} %refs_2_.1, bf16[192,4096]{1,0:T(8,128)(2,1)} %refs_3_.1, bf16[192,4096]{1,0:T(8,128)(2,1)} %refs_4_.1, bf16[192,4096]{1,0:T(8,128)(2,1)} %refs_5_.1), custom_call_target="tpu_custom_call" | custom-call | flops 226492416 | bytes 4718592 | tf_op jit(solution)/shard_map/tails/pallas_call | solution.py:151
  15.4 0.1 collective-permute-start.4
  15.5 1.5 %fusion.15 = (f32[1]{0:T(128)}, f32[1]{0:T(128)}, f32[1]{0:T(128)}, f32[1]{0:T(128)}, f32[1]{0:T(128)}) fusion(f32[8]{0:T(128)} %get-tuple-element.23), kind=kLoop, calls=%fused_computation.21 | loop fusion | bytes 40 | tf_op jit(solution)/shard_map/slice | solution.py:220
  17.0 0.0 collective-permute-done
  17.0 0.0 copy-done.1
  17.0 0.8 fusion.7
  17.8 2.1 %collective-permute-start.1 = (bf16[14,128,128]{2,1,0:T(8,128)(2,1)S(1)}, bf16[14,128,128]{2,1,0:T(8,128)(2,1)S(1)}, u32[]{:S(2)}, u32[]{:S(2)}) collective-permute-start(bf16[14,128,128]{2,1,0:T(8,128)(2,1)S(1)} %fusion.7), channel_id=1, source_target_pairs={{0,4},{2,6},{4,8},{5,1},{6,10},{7,3},{8,12},{9,5},{10,14},{11,7},{... | collective-permute-start | bytes 1376264 | tf_op jit(solution)/shard_map/ppermute | solution.py:202
  19.9 0.0 collective-permute-done.4
  20.0 0.9 fusion.1
  20.9 2.1 %collective-permute-start.5 = (bf16[18,128,128]{2,1,0:T(8,128)(2,1)S(1)}, bf16[18,128,128]{2,1,0:T(8,128)(2,1)S(1)}, u32[]{:S(2)}, u32[]{:S(2)}) collective-permute-start(bf16[18,128,128]{2,1,0:T(8,128)(2,1)S(1)} %fusion.1), channel_id=1, source_target_pairs={{0,2},{2,4},{3,1},{4,6},{5,3},{6,8},{7,5},{8,10},{9,7},{10,12},{11... | collective-permute-start | bytes 1769480 | tf_op jit(solution)/shard_map/ppermute | solution.py:202
  23.0 4.4 %collective-permute-done.1 = bf16[14,128,128]{2,1,0:T(8,128)(2,1)S(1)} collective-permute-done((bf16[14,128,128]{2,1,0:T(8,128)(2,1)S(1)}, bf16[14,128,128]{2,1,0:T(8,128)(2,1)S(1)}, u32[]{:S(2)}, u32[]{:S(2)}) %collective-permute-start.1) | collective-permute-done | bytes 458784 | tf_op jit(solution)/shard_map/ppermute | solution.py:202
  27.4 0.8 fusion.10
  28.1 8.0 %collective-permute-done.5 = bf16[18,128,128]{2,1,0:T(8,128)(2,1)S(1)} collective-permute-done((bf16[18,128,128]{2,1,0:T(8,128)(2,1)S(1)}, bf16[18,128,128]{2,1,0:T(8,128)(2,1)S(1)}, u32[]{:S(2)}, u32[]{:S(2)}) %collective-permute-start.5) | collective-permute-done | bytes 589856 | tf_op jit(solution)/shard_map/ppermute | solution.py:202
  36.1 0.8 fusion.4
  37.0 1.9 %collective-permute-start.6 = (bf16[18,128,128]{2,1,0:T(8,128)(2,1)S(1)}, bf16[18,128,128]{2,1,0:T(8,128)(2,1)S(1)}, u32[]{:S(2)}, u32[]{:S(2)}) collective-permute-start(bf16[18,128,128]{2,1,0:T(8,128)(2,1)S(1)} %fusion.4), channel_id=1, source_target_pairs={{0,4},{2,6},{4,8},{5,1},{6,10},{7,3},{8,12},{9,5},{10,14},{11,7},{... | collective-permute-start | bytes 1769480 | tf_op jit(solution)/shard_map/ppermute | solution.py:202
  38.9 3.8 %collective-permute-start.2 = (bf16[14,128,128]{2,1,0:T(8,128)(2,1)S(1)}, bf16[14,128,128]{2,1,0:T(8,128)(2,1)S(1)}, u32[]{:S(2)}, u32[]{:S(2)}) collective-permute-start(bf16[14,128,128]{2,1,0:T(8,128)(2,1)S(1)} %fusion.10), channel_id=1, source_target_pairs={{0,2},{2,4},{3,1},{4,6},{5,3},{6,8},{7,5},{8,10},{9,7},{10,12},{11... | collective-permute-start | bytes 1376264 | tf_op jit(solution)/shard_map/ppermute | solution.py:202
  42.7 5.2 %collective-permute-done.6 = bf16[18,128,128]{2,1,0:T(8,128)(2,1)S(1)} collective-permute-done((bf16[18,128,128]{2,1,0:T(8,128)(2,1)S(1)}, bf16[18,128,128]{2,1,0:T(8,128)(2,1)S(1)}, u32[]{:S(2)}, u32[]{:S(2)}) %collective-permute-start.6) | collective-permute-done | bytes 589856 | tf_op jit(solution)/shard_map/ppermute | solution.py:202
  47.9 2.4 %fusion.2 = (bf16[18,128,128]{2,1,0:T(8,128)(2,1)S(1)}, bf16[18,128,128]{2,1,0:T(8,128)(2,1)}) fusion(bf16[18,128,128]{2,1,0:T(8,128)(2,1)S(1)} %copy-done, f32[]{:T(128)} %bitcast.4, bf16[18,128,128]{2,1,0:T(8,128)(2,1)S(1)} %collective-permute-done.6, f32[]{:T(128)} %bitcast.3, bf16[18,128,128]{2,1,0:T(8,128)(2,1)S(1)} %collective-permute-done.5), kind=kLoop, calls=%fused_computation.6 | loop fusion | flops 2949120 | bytes 2949128 | tf_op jit(solution)/shard_map/convert_element_type | solution.py:205
  50.3 5.1 %collective-permute-start.7 = (bf16[18,128,128]{2,1,0:T(8,128)(2,1)S(1)}, bf16[18,128,128]{2,1,0:T(8,128)(2,1)S(1)}, u32[]{:S(2)}, u32[]{:S(2)}) collective-permute-start(bf16[18,128,128]{2,1,0:T(8,128)(2,1)S(1)} %get-tuple-element.40), channel_id=1, source_target_pairs={{0,1},{1,0},{2,3},{3,2},{4,5},{5,4},{6,7},{7,6},{8,9},{9,8},{10,11... | collective-permute-start | bytes 1769480 | tf_op jit(solution)/shard_map/ppermute | solution.py:198
  55.4 0.0 collective-permute-done.2
  55.4 2.3 %fusion.8 = (bf16[14,128,128]{2,1,0:T(8,128)(2,1)S(1)}, bf16[14,128,128]{2,1,0:T(8,128)(2,1)}) fusion(bf16[14,128,128]{2,1,0:T(8,128)(2,1)S(1)} %copy-done.1, f32[]{:T(128)} %bitcast.4, bf16[14,128,128]{2,1,0:T(8,128)(2,1)S(1)} %collective-permute-done.1, f32[]{:T(128)} %bitcast.3, bf16[14,128,128]{2,1,0:T(8,128)(2,1)S(1)} %collective-permute-done.2), kind=kLoop, calls=%fused_computation.16 | loop fusion | flops 2293760 | bytes 2293768 | tf_op jit(solution)/shard_map/convert_element_type | solution.py:205
  57.7 4.4 %collective-permute-start.3 = (bf16[14,128,128]{2,1,0:T(8,128)(2,1)S(1)}, bf16[14,128,128]{2,1,0:T(8,128)(2,1)S(1)}, u32[]{:S(2)}, u32[]{:S(2)}) collective-permute-start(bf16[14,128,128]{2,1,0:T(8,128)(2,1)S(1)} %get-tuple-element.42), channel_id=1, source_target_pairs={{0,1},{1,0},{2,3},{3,2},{4,5},{5,4},{6,7},{7,6},{8,9},{9,8},{10,11... | collective-permute-start | bytes 1376264 | tf_op jit(solution)/shard_map/ppermute | solution.py:198
  62.0 8.5 %local.2 = (bf16[192,1792]{1,0:T(8,128)(2,1)}, bf16[192,1792]{1,0:T(8,128)(2,1)}, bf16[192,1792]{1,0:T(8,128)(2,1)}, bf16[192,1792]{1,0:T(8,128)(2,1)}) custom-call(s32[1]{0:T(128)} %bitcast.pos_ref.refs_0_, s32[4]{0:T(128)} %refs_1_.1, bf16[192,4096]{1,0:T(8,128)(2,1)} %refs_2_.1, bf16[192,4096]{1,0:T(8,128)(2,1)} %refs_3_.1, bf16[192,4096]{1,0:T(8,128)(2,1)} %refs_4_.1, ...), custom_call_target="tpu_custom_call" | custom-call | flops 792723456 | bytes 5505024 | tf_op jit(solution)/shard_map/local/pallas_call | solution.py:163
  70.5 10.5 %local.3 = (bf16[192,2304]{1,0:T(8,128)(2,1)}, bf16[192,2304]{1,0:T(8,128)(2,1)}, bf16[192,2304]{1,0:T(8,128)(2,1)}, bf16[192,2304]{1,0:T(8,128)(2,1)}) custom-call(s32[1]{0:T(128)} %bitcast.pos_ref.refs_0_, s32[4]{0:T(128)} %refs_1_.1, bf16[192,4096]{1,0:T(8,128)(2,1)} %refs_2_.1, bf16[192,4096]{1,0:T(8,128)(2,1)} %refs_3_.1, bf16[192,4096]{1,0:T(8,128)(2,1)} %refs_4_.1, ...), custom_call_target="tpu_custom_call" | custom-call | flops 1019215872 | bytes 7077888 | tf_op jit(solution)/shard_map/local/pallas_call | solution.py:163
  81.0 0.0 collective-permute-done.7.other_ref
  81.0 0.8 copy-done.2
  81.8 9.1 %final.2 = (bf16[192,4096]{1,0:T(8,128)(2,1)}, bf16[192,4096]{1,0:T(8,128)(2,1)}, bf16[192,4096]{1,0:T(8,128)(2,1)}, bf16[192,4096]{1,0:T(8,128)(2,1)}) custom-call(s32[1]{0:T(128)} %bitcast.pos_ref.refs_0_, s32[4]{0:T(128)} %refs_1_.1, bf16[192,4096]{1,0:T(8,128)(2,1)} %refs_2_.1, bf16[192,4096]{1,0:T(8,128)(2,1)} %refs_3_.1, bf16[192,4096]{1,0:T(8,128)(2,1)} %refs_4_.1, ...), custom_call_target="tpu_custom_call" | custom-call | flops 452984832 | bytes 10616832 | tf_op jit(solution)/shard_map/final/pallas_call | solution.py:185
  90.9 0.0 collective-permute-done.3.refs_7_
  90.9 0.8 copy-done.3
  91.7 7.5 %final.3 = (bf16[192,4096]{1,0:T(8,128)(2,1)}, bf16[192,4096]{1,0:T(8,128)(2,1)}, bf16[192,4096]{1,0:T(8,128)(2,1)}, bf16[192,4096]{1,0:T(8,128)(2,1)}) custom-call(s32[1]{0:T(128)} %bitcast.pos_ref.refs_0_, s32[4]{0:T(128)} %refs_1_.1, bf16[192,4096]{1,0:T(8,128)(2,1)} %refs_2_.1, ...), custom_call_target="tpu_custom_call", output_to_operand_aliasing={{0}: (12, {}), {1}: (13, {}), {2}: (14, {}), {3}: (15, {})} | custom-call | flops 352321536 | bytes 8257536 | tf_op jit(solution)/shard_map/final/pallas_call | solution.py:185
  (5 shorter events, 0.0 us)
Async XLA Ops:
  6.9 10.1 %copy-start.1 = (bf16[14,128,128]{2,1,0:T(8,128)(2,1)S(1)}, bf16[14,128,128]{2,1,0:T(8,128)(2,1)}, u32[]{:S(2)}) copy-start(bf16[14,128,128]{2,1,0:T(8,128)(2,1)} %get-tuple-element.24) | copy-start | bytes 1376260
  6.9 10.1 %collective-permute-start = (bf16[14,128,128]{2,1,0:T(8,128)(2,1)}, bf16[14,128,128]{2,1,0:T(8,128)(2,1)S(1)}, u32[]{:S(2)}, u32[]{:S(2)}) collective-permute-start(bf16[14,128,128]{2,1,0:T(8,128)(2,1)} %get-tuple-element.22), channel_id=1, source_target_pairs={{0,1},{1,0},{2,3},{3,2},{4,5},{5,4},{6,7},{7,6},{8,9},{9,8},{10,11... | collective-permute-start | bytes 1376264 | tf_op jit(solution)/shard_map/ppermute | solution.py:198
  15.4 4.6 %copy-start = (bf16[18,128,128]{2,1,0:T(8,128)(2,1)S(1)}, bf16[18,128,128]{2,1,0:T(8,128)(2,1)}, u32[]{:S(2)}) copy-start(bf16[18,128,128]{2,1,0:T(8,128)(2,1)} %get-tuple-element.30) | copy-start | bytes 1769476
  15.4 4.6 %collective-permute-start.4 = (bf16[18,128,128]{2,1,0:T(8,128)(2,1)}, bf16[18,128,128]{2,1,0:T(8,128)(2,1)S(1)}, u32[]{:S(2)}, u32[]{:S(2)}) collective-permute-start(bf16[18,128,128]{2,1,0:T(8,128)(2,1)} %get-tuple-element.29), channel_id=1, source_target_pairs={{0,1},{1,0},{2,3},{3,2},{4,5},{5,4},{6,7},{7,6},{8,9},{9,8},{10,11... | collective-permute-start | bytes 1769480 | tf_op jit(solution)/shard_map/ppermute | solution.py:198
  17.8 9.5 %collective-permute-start.1 = (bf16[14,128,128]{2,1,0:T(8,128)(2,1)S(1)}, bf16[14,128,128]{2,1,0:T(8,128)(2,1)S(1)}, u32[]{:S(2)}, u32[]{:S(2)}) collective-permute-start(bf16[14,128,128]{2,1,0:T(8,128)(2,1)S(1)} %fusion.7), channel_id=1, source_target_pairs={{0,4},{2,6},{4,8},{5,1},{6,10},{7,3},{8,12},{9,5},{10,14},{11,7},{... | collective-permute-start | bytes 1376264 | tf_op jit(solution)/shard_map/ppermute | solution.py:202
  20.9 15.3 %collective-permute-start.5 = (bf16[18,128,128]{2,1,0:T(8,128)(2,1)S(1)}, bf16[18,128,128]{2,1,0:T(8,128)(2,1)S(1)}, u32[]{:S(2)}, u32[]{:S(2)}) collective-permute-start(bf16[18,128,128]{2,1,0:T(8,128)(2,1)S(1)} %fusion.1), channel_id=1, source_target_pairs={{0,2},{2,4},{3,1},{4,6},{5,3},{6,8},{7,5},{8,10},{9,7},{10,12},{11... | collective-permute-start | bytes 1769480 | tf_op jit(solution)/shard_map/ppermute | solution.py:202
  37.0 10.9 %collective-permute-start.6 = (bf16[18,128,128]{2,1,0:T(8,128)(2,1)S(1)}, bf16[18,128,128]{2,1,0:T(8,128)(2,1)S(1)}, u32[]{:S(2)}, u32[]{:S(2)}) collective-permute-start(bf16[18,128,128]{2,1,0:T(8,128)(2,1)S(1)} %fusion.4), channel_id=1, source_target_pairs={{0,4},{2,6},{4,8},{5,1},{6,10},{7,3},{8,12},{9,5},{10,14},{11,7},{... | collective-permute-start | bytes 1769480 | tf_op jit(solution)/shard_map/ppermute | solution.py:202
  38.9 16.5 %collective-permute-start.2 = (bf16[14,128,128]{2,1,0:T(8,128)(2,1)S(1)}, bf16[14,128,128]{2,1,0:T(8,128)(2,1)S(1)}, u32[]{:S(2)}, u32[]{:S(2)}) collective-permute-start(bf16[14,128,128]{2,1,0:T(8,128)(2,1)S(1)} %fusion.10), channel_id=1, source_target_pairs={{0,2},{2,4},{3,1},{4,6},{5,3},{6,8},{7,5},{8,10},{9,7},{10,12},{11... | collective-permute-start | bytes 1376264 | tf_op jit(solution)/shard_map/ppermute | solution.py:202
  50.3 30.7 %collective-permute-start.7 = (bf16[18,128,128]{2,1,0:T(8,128)(2,1)S(1)}, bf16[18,128,128]{2,1,0:T(8,128)(2,1)S(1)}, u32[]{:S(2)}, u32[]{:S(2)}) collective-permute-start(bf16[18,128,128]{2,1,0:T(8,128)(2,1)S(1)} %get-tuple-element.40), channel_id=1, source_target_pairs={{0,1},{1,0},{2,3},{3,2},{4,5},{5,4},{6,7},{7,6},{8,9},{9,8},{10,11... | collective-permute-start | bytes 1769480 | tf_op jit(solution)/shard_map/ppermute | solution.py:198
  57.7 33.2 %collective-permute-start.3 = (bf16[14,128,128]{2,1,0:T(8,128)(2,1)S(1)}, bf16[14,128,128]{2,1,0:T(8,128)(2,1)S(1)}, u32[]{:S(2)}, u32[]{:S(2)}) collective-permute-start(bf16[14,128,128]{2,1,0:T(8,128)(2,1)S(1)} %get-tuple-element.42), channel_id=1, source_target_pairs={{0,1},{1,0},{2,3},{3,2},{4,5},{5,4},{6,7},{7,6},{8,9},{9,8},{10,11... | collective-permute-start | bytes 1376264 | tf_op jit(solution)/shard_map/ppermute | solution.py:198
  81.0 0.8 copy-start.2
  90.9 0.8 copy-start.3

commit v2 on v1

v2 whole, which is shorter than its diff:
```python
import functools
import math

import jax
import jax.numpy as jnp
from jax import lax
from jax.experimental import pallas as pl
from jax.experimental.pallas import tpu as pltpu
from jax.sharding import PartitionSpec as P

DH = 128
UNIT = 128
LONGEST = 10
N_X = 18
N_GAP = 4
F32 = jnp.float32
BF16 = jnp.bfloat16


def doc_of(pos, doc_ref, docs):
    count = jnp.int32(0)
    end = jnp.int32(0)
    for d in range(docs):
        end = end + doc_ref[d] * UNIT
        count = count + (pos >= end).astype(jnp.int32)
    return jnp.where(pos < 0, jnp.int32(-1), count)


def edges(pos_ref, doc_ref, rows, docs):
    first = pos_ref[0] * rows
    start = jnp.int32(0)
    stop = jnp.int32(1 << 30)
    end = jnp.int32(0)
    for d in range(docs):
        end = end + doc_ref[d] * UNIT
        start = jnp.where(end <= first + (rows - 1), end, start)
        stop = jnp.minimum(stop, jnp.where(end > first, end, jnp.int32(1 << 30)))
    return start - first, stop - first


def dot_tt(a, b):
    return lax.dot_general(a, b, (((0,), (0,)), ((), ())), preferred_element_type=F32)


def dot_nt(a, b):
    return lax.dot_general(a, b, (((1,), (1,)), ((), ())), preferred_element_type=F32)


def dot_nn(a, b):
    return lax.dot_general(a, b, (((1,), (0,)), ((), ())), preferred_element_type=F32)


def tails_of(pos_ref, doc_ref, q_ref, k_ref, v_ref, g_ref, keep_ref, send_ref, lo, sizes, docs, ready=None):
    rows = q_ref.shape[0]
    even = lax.rem(pos_ref[0], 2) == 0
    start, stop = edges(pos_ref, doc_ref, rows, docs)
    row = lax.broadcasted_iota(jnp.int32, (rows, DH), 0)
    in_tail = row >= start
    in_head = row < stop
    zero = jnp.zeros((), BF16)
    at = 0
    for c, size in enumerate(sizes):
        if ready is not None:
            ready(c)
        for i in range(at, at + size):
            cols = pl.ds((lo + i) * DH, DH)
            tail = dot_tt(jnp.where(in_tail, k_ref[:, cols], zero), v_ref[:, cols]).astype(BF16)
            head = dot_tt(jnp.where(in_head, q_ref[:, cols], zero), g_ref[:, cols]).astype(BF16)
            keep_ref[i] = jnp.where(even, tail, head)
            send_ref[i] = jnp.where(even, head, tail)
        at += size


def open_kernel(pos_ref, doc_ref, q_hbm, k_hbm, v_hbm, g_hbm, q_ref, k_ref, v_ref, g_ref, keep_ref, send_ref, w_ref, sems, *, docs, sizes):
    rows, width = q_ref.shape
    dev = pos_ref[0]
    core = lax.rem(dev, 2)
    arrays = ((k_hbm, k_ref), (v_hbm, v_ref), (q_hbm, q_ref), (g_hbm, g_ref))
    rest = width // DH - sum(sizes)
    copies = []
    at = 0
    for c, size in enumerate((*sizes, rest)):
        cols = pl.ds(at * DH, size * DH)
        group = [pltpu.make_async_copy(src.at[:, cols], dst.at[:, cols], sems.at[c, a]) for a, (src, dst) in enumerate(arrays)]
        for cp in group:
            cp.start()
        copies.append(group)
        at += size
    chip = dev - core

    def key(u):
        pos = jnp.where(core == 0, rows * (chip + 2 - u) - 1, rows * (chip + u))
        return doc_of(pos, doc_ref, docs)

    k0, k1, k2, k4 = key(0), key(1), key(2), key(4)
    same = (k1 == k0, k2 == k0, k4 == k2, k4 == k0, k2 == k1)
    for i, flag in enumerate(same):
        w_ref[i] = flag.astype(F32)
    for i in range(len(same), 8):
        w_ref[i] = jnp.float32(0)

    def ready(c):
        for cp in copies[c]:
            cp.wait()

    tails_of(pos_ref, doc_ref, q_ref, k_ref, v_ref, g_ref, keep_ref, send_ref, 0, sizes, docs, ready)
    ready(len(sizes))


def tails_kernel(pos_ref, doc_ref, q_ref, k_ref, v_ref, g_ref, keep_ref, send_ref, *, docs, lo, n):
    tails_of(pos_ref, doc_ref, q_ref, k_ref, v_ref, g_ref, keep_ref, send_ref, lo, (n,), docs)


def local_kernel(pos_ref, doc_ref, q_ref, k_ref, v_ref, g_ref, o_ref, dq_ref, dk_ref, dv_ref, *, docs, lo, n, scale, unroll):
    rows = q_ref.shape[0]
    start, _ = edges(pos_ref, doc_ref, rows, docs)
    t = lax.broadcasted_iota(jnp.int32, (rows, rows), 0)
    s = lax.broadcasted_iota(jnp.int32, (rows, rows), 1)
    allowed = (s <= t) & ((t < start) | (s >= start))

    def step(j, carry):
        for u in range(unroll):
            i = j * unroll + u
            src = pl.ds(pl.multiple_of((lo + i) * DH, DH), DH)
            dst = pl.ds(pl.multiple_of(i * DH, DH), DH)
            q, k, v, g = q_ref[:, src], k_ref[:, src], v_ref[:, src], g_ref[:, src]
            probs = jnp.where(allowed, dot_nt(q, k), 0.0).astype(BF16)
            dprobs = jnp.where(allowed, dot_nt(g, v), 0.0).astype(BF16)
            o_ref[:, dst] = (scale * dot_nn(probs, v)).astype(BF16)
            dq_ref[:, dst] = (scale * dot_nn(dprobs, k)).astype(BF16)
            dk_ref[:, dst] = (scale * dot_tt(dprobs, q)).astype(BF16)
            dv_ref[:, dst] = (scale * dot_tt(probs, g)).astype(BF16)
        return carry

    lax.fori_loop(0, n // unroll, step, 0)


def final_kernel(pos_ref, doc_ref, q_ref, k_ref, v_ref, g_ref, mine_ref, other_ref, parts, outs, bufs, sems, *, docs, lo, sizes, scale):
    rows = q_ref.shape[0]
    dev = pos_ref[0]
    forward = lax.rem(dev, 2) == 0
    first = dev * rows
    prev_doc = doc_of(first - 1, doc_ref, docs)
    next_doc = doc_of(first + rows, doc_ref, docs)
    first_doc = doc_of(first, doc_ref, docs)
    last_doc = doc_of(first + (rows - 1), doc_ref, docs)
    start, stop = edges(pos_ref, doc_ref, rows, docs)
    row = lax.broadcasted_iota(jnp.int32, (rows, DH), 0)
    into = jnp.where(first_doc == prev_doc, stop, 0)
    onto = jnp.where(last_doc == next_doc, start, rows)
    reads = row < into
    feeds = row >= onto
    copies = []
    at = 0
    for c, size in enumerate(sizes):
        for i in range(at, at + size):
            cols = pl.ds(i * DH, DH)
            src = pl.ds((lo + i) * DH, DH)
            q, k, v, g = q_ref[:, src], k_ref[:, src], v_ref[:, src], g_ref[:, src]
            state = jnp.where(forward, mine_ref[i], other_ref[i])
            back = jnp.where(forward, other_ref[i], mine_ref[i])
            terms = ((reads, dot_nn(q, state)), (reads, dot_nt(g, state)), (feeds, dot_nt(v, back)), (feeds, dot_nn(k, back)))
            piece, rel = 0, i
            while rel * DH >= parts[piece].shape[1]:
                rel -= parts[piece].shape[1] // DH
                piece += 4
            inner = pl.ds(rel * DH, DH)
            for a, (mask, term) in enumerate(terms):
                bufs[a][:, cols] = (parts[piece + a][:, inner].astype(F32) + jnp.where(mask, scale * term, 0.0)).astype(BF16)
        for a in range(4):
            cp = pltpu.make_async_copy(
                bufs[a].at[:, pl.ds(at * DH, size * DH)],
                outs[a].at[:, pl.ds((lo + at) * DH, size * DH)],
                sems.at[c, a],
            )
            cp.start()
            copies.append(cp)
        at += size
    for cp in copies:
        cp.wait()


def plus_kernel(flag_ref, base_ref, x_ref, out_ref, *, which):
    flag = jnp.full(base_ref.shape[1:], flag_ref[which], F32).astype(BF16)
    for i in range(base_ref.shape[0]):
        out_ref[i] = base_ref[i] + flag * x_ref[i]


def close_kernel(flag_ref, near_ref, far_ref, keep_ref, mine_ref, pass_ref, *, one, two):
    flag = jnp.full(near_ref.shape[1:], flag_ref[one], F32).astype(BF16)
    flag2 = jnp.full(near_ref.shape[1:], flag_ref[two], F32).astype(BF16)
    for i in range(near_ref.shape[0]):
        mine = near_ref[i] + flag * far_ref[i]
        mine_ref[i] = mine
        pass_ref[i] = keep_ref[i] + flag2 * mine


def split(n, size):
    return (size,) * (n // size) + ((n % size,) if n % size else ())


def on_device(queries, keys, values, out_grad, doc_blocks):
    rows, width = queries.shape
    n_heads = width // DH
    docs = doc_blocks.shape[0]
    devices = lax.axis_size("seq")
    scale = 1.0 / math.sqrt(DH * n_heads * LONGEST)
    dev = lax.axis_index("seq").astype(jnp.int32).reshape(1)
    smem = pl.BlockSpec(memory_space=pltpu.SMEM)
    vmem = pl.BlockSpec(memory_space=pltpu.VMEM)
    hbm = pl.BlockSpec(memory_space=pltpu.HBM)
    params = pltpu.CompilerParams(vmem_limit_bytes=24 << 20)
    cost = pl.CostEstimate(flops=1024, transcendentals=0, bytes_accessed=1024)

    def shaped(*shape):
        return jax.ShapeDtypeStruct(shape, BF16)

    def opened(n):
        sizes = split(n, 4)
        out = pl.pallas_call(
            functools.partial(open_kernel, docs=docs, sizes=sizes),
            in_specs=[smem, smem] + [hbm] * 4,
            out_specs=[vmem] * 6 + [smem],
            out_shape=[shaped(rows, width)] * 4 + [shaped(n, DH, DH)] * 2 + [jax.ShapeDtypeStruct((8,), F32)],
            scratch_shapes=[pltpu.SemaphoreType.DMA((len(sizes) + 1, 4))],
            compiler_params=pltpu.CompilerParams(vmem_limit_bytes=46 << 20),
            cost_estimate=cost,
            name="opened",
        )(dev, doc_blocks, queries, keys, values, out_grad)
        return out[:4], out[4], out[5], out[6]

    def tails(blocks, lo, n):
        return pl.pallas_call(
            functools.partial(tails_kernel, docs=docs, lo=lo, n=n),
            in_specs=[smem, smem] + [vmem] * 4,
            out_specs=[vmem] * 2,
            out_shape=[shaped(n, DH, DH)] * 2,
            compiler_params=params,
            cost_estimate=cost,
            name="tails",
        )(dev, doc_blocks, *blocks)

    def local(blocks, lo, n, flops=1024):
        return pl.pallas_call(
            functools.partial(local_kernel, docs=docs, lo=lo, n=n, scale=scale, unroll=2),
            in_specs=[smem, smem] + [vmem] * 4,
            out_specs=[vmem] * 4,
            out_shape=[shaped(rows, n * DH)] * 4,
            compiler_params=params,
            cost_estimate=pl.CostEstimate(flops=flops, transcendentals=0, bytes_accessed=1024),
            name="local",
        )(dev, doc_blocks, *blocks)

    def final(blocks, lo, n, mine, other, parts, outs):
        aliased = [] if outs is None else list(outs)
        sizes = split(n, 4)
        first_alias = 8 + len(parts)

        def body(*refs):
            ins, rest = refs[:first_alias], refs[first_alias + len(aliased) :]
            final_kernel(*ins[:8], ins[8:], rest[:4], rest[4:8], rest[8], docs=docs, lo=lo, sizes=sizes, scale=scale)

        return pl.pallas_call(
            body,
            in_specs=[smem, smem] + [vmem] * (6 + len(parts)) + [hbm] * len(aliased),
            out_specs=[hbm] * 4,
            out_shape=[shaped(rows, width)] * 4,
            scratch_shapes=[pltpu.VMEM((rows, n * DH), BF16)] * 4 + [pltpu.SemaphoreType.DMA((len(sizes), 4))],
            input_output_aliases={first_alias + i: i for i in range(len(aliased))},
            compiler_params=params,
            cost_estimate=cost,
            name="final",
        )(dev, doc_blocks, *blocks, mine, other, *parts, *aliased)

    def across(x):
        return lax.ppermute(x, "seq", [(i, i ^ 1) for i in range(devices)])

    def along(x, by):
        pairs = [(i, i + by if i % 2 == 0 else i - by) for i in range(devices)]
        return lax.ppermute(x, "seq", [(i, j) for i, j in pairs if 0 <= j < devices])

    def plus(base, which, x):
        return pl.pallas_call(
            functools.partial(plus_kernel, which=which),
            in_specs=[smem] + [vmem] * 2,
            out_specs=vmem,
            out_shape=shaped(*base.shape),
            compiler_params=params,
            cost_estimate=cost,
            name="plus",
        )(flags, base, x)

    def close(near, far, keep):
        return pl.pallas_call(
            functools.partial(close_kernel, one=2, two=4),
            in_specs=[smem] + [vmem] * 3,
            out_specs=[vmem] * 2,
            out_shape=[shaped(*near.shape)] * 2,
            compiler_params=params,
            cost_estimate=cost,
            name="close",
        )(flags, near, far, keep)

    n_w = n_heads - N_X
    blocks, keep_x, send_x, flags = opened(N_X)
    keep_w, send_w = tails(blocks, N_X, n_w)
    total_x = plus(across(send_x), 0, keep_x)
    total_w = plus(across(send_w), 0, keep_w)
    near_x = along(total_x, 2)
    far_w = along(total_w, 4)
    part_w = local(blocks, N_X, n_w, 1024)
    far_w, part_w = lax.optimization_barrier((far_w, part_w))
    gathered_w = plus(total_w, 3, far_w)
    near_w = along(gathered_w, 2)
    later, _ = lax.optimization_barrier((blocks, gathered_w))
    part_x = local(later, 0, N_GAP, 1024)
    near_x, part_x = lax.optimization_barrier((near_x, part_x))
    gathered_x = plus(total_x, 1, near_x)
    far_x = along(gathered_x, 4)
    later, _ = lax.optimization_barrier((blocks, gathered_x))
    part_y = local(later, N_GAP, N_X - N_GAP, 10**10)
    far_x, part_y = lax.optimization_barrier((far_x, part_y))
    mine_x, pass_x = close(near_x, far_x, keep_x)
    mine_w, pass_w = close(near_w, far_w, keep_w)
    other_x = across(pass_x)
    other_w = across(pass_w)
    outs = final(blocks, 0, N_X, mine_x, other_x, (*part_x, *part_y), None)
    outs = final(blocks, N_X, n_w, mine_w, other_w, part_w, outs)
    return tuple(outs)


def solution(mesh):
    spec = P(("sweep", "seq"), None)
    return jax.shard_map(
        on_device,
        mesh=mesh,
        in_specs=(spec, spec, spec, spec, P("sweep")),
        out_specs=(spec, spec, spec, spec),
        check_vma=False,
    )
```

time: 101 us -> 54.2 us (0.54)
  the two profiles are of different devices: /device:TPU:15 before, /device:TPU:1 now
where the time goes in v2:
time: 54.2 us; the launch traced here: 53.6 us
  Pallas kernels  31.2 us (58%)
  waiting for transfers between devices  12.8 us (24%)
  starting transfers between devices  8.24 us (15%)
  between operations  0.78 us (1%)
  local copies, waits for them, and re-layouts  0.65 us (1%)
    pallas_call x3, Pallas kernels, local(): pl.pallas_call(functools.partial(local_kernel, docs=docs, lo=lo, n=n, sca...  14.7 us
    ppermute x4, waiting for transfers between devices, along(): lax.ppermute(x, 'seq', [(i, j) for i, j in pairs if 0 <= j < devices])  11.9 us
    pallas_call x2, Pallas kernels, final(): pl.pallas_call(body, in_specs=[smem, smem] + [vmem] * (6 + len(parts)) +...  6.74 us
    ppermute x4, starting transfers between devices, along(): lax.ppermute(x, 'seq', [(i, j) for i, j in pairs if 0 <= j < devices])  5.17 us
    pallas_call x1, Pallas kernels, opened(): pl.pallas_call(functools.partial(open_kernel, docs=docs, sizes=sizes), in...  4.35 us
    ppermute x4, starting transfers between devices, across(): return lax.ppermute(x, 'seq', [(i, i ^ 1) for i in range(devices)])  3.07 us
    pallas_call x4, Pallas kernels, plus(): pl.pallas_call(functools.partial(plus_kernel, which=which), in_specs=[sme...  2.65 us
    pallas_call x2, Pallas kernels, close(): pl.pallas_call(functools.partial(close_kernel, one=2, two=4), in_specs=[s...  1.49 us
  transfers between devices with their start and end apart: 8, of which 4 were waited for; matrix products, arithmetic and copies ran while one was open for 0% of the time, Pallas kernels for 44%

profile of v2, /device:TPU:1, one launch (start us, length us, event | category | flops | bytes accessed | tf_op | source)
XLA Modules:
  0.0 53.6 jit_solution(7491648780624783860)
XLA Ops:
  0.6 0.0 copy-start
  0.6 0.6 %copy-done = s32[4]{0:T(128)S(1)} copy-done((s32[4]{0:T(128)S(1)}, s32[4]{0:T(128)}, u32[]{:S(2)}) %copy-start) | copy-done | bytes 40
  1.3 4.3 %opened.1 = (bf16[192,4096]{1,0:T(8,128)(2,1)S(1)}, bf16[192,4096]{1,0:T(8,128)(2,1)S(1)}, bf16[192,4096]{1,0:T(8,128)(2,1)S(1)}, bf16[192,4096]{1,0:T(8,128)(2,...) custom-call(s32[1]{0:T(128)} %bitcast.pos_ref.refs_0_, s32[4]{0:T(128)S(1)} %copy-done, ...), custom_call_target="tpu_custom_call" | custom-call | flops 1024 | bytes 1024 | tf_op jit(solution)/shard_map/opened/pallas_call | solution.py:220
  5.7 0.1 collective-permute-start.4
  5.7 1.3 %tails.1 = (bf16[14,128,128]{2,1,0:T(8,128)(2,1)S(1)}, bf16[14,128,128]{2,1,0:T(8,128)(2,1)S(1)}) custom-call(s32[1]{0:T(128)} %bitcast.pos_ref.refs_0_, s32[4]{0:T(128)S(1)} %copy-done, bf16[192,4096]{1,0:T(8,128)(2,1)S(1)} %get-tuple-element.85.q_ref.refs_2_, bf16[192,4096]{1,0:T(8,128)(2,1)S(1)} %get-tuple-element.86.k_ref.refs_3_, ...), custom_call_target="tpu_custom_call" | custom-call | flops 1024 | bytes 1024 | tf_op jit(solution)/shard_map/tails/pallas_call | solution.py:233
  7.1 0.6 %collective-permute-start = (bf16[14,128,128]{2,1,0:T(8,128)(2,1)S(1)}, bf16[14,128,128]{2,1,0:T(8,128)(2,1)S(1)}, u32[]{:S(2)}, u32[]{:S(2)}) collective-permute-start(bf16[14,128,128]{2,1,0:T(8,128)(2,1)S(1)} %get-tuple-element.61), channel_id=1, source_target_pairs={{0,1},{1,0},{2,3},{3,2},{4,5},{5,4},{6,7},{7,6},{8,9},{9,8},{10,11... | collective-permute-start | bytes 1376264 | tf_op jit(solution)/shard_map/ppermute | solution.py:276
  7.6 0.1 collective-permute-done.4.base_ref
  7.7 0.7 %plus.6.base_ref = bf16[18,128,128]{2,1,0:T(8,128)(2,1)S(1)} custom-call(f32[8]{0:T(128)S(1)} %get-tuple-element.60.flag_ref, bf16[18,128,128]{2,1,0:T(8,128)(2,1)S(1)} %collective-permute-done.4.base_ref, bf16[18,128,128]{2,1,0:T(8,128)(2,1)S(1)} %get-tuple-element.75.x_ref.keep_ref), custom_call_target="tpu_custom_call" | custom-call | flops 1024 | bytes 1024 | tf_op jit(solution)/shard_map/plus/pallas_call | solution.py:283
  8.4 1.3 %collective-permute-start.5 = (bf16[18,128,128]{2,1,0:T(8,128)(2,1)S(1)}, bf16[18,128,128]{2,1,0:T(8,128)(2,1)S(1)}, u32[]{:S(2)}, u32[]{:S(2)}) collective-permute-start(bf16[18,128,128]{2,1,0:T(8,128)(2,1)S(1)} %plus.6.base_ref), channel_id=1, source_target_pairs={{0,2},{2,4},{3,1},{4,6},{5,3},{6,8},{7,5},{8,10},{9,7},{10,12},{11... | collective-permute-start | bytes 1769480 | tf_op jit(solution)/shard_map/ppermute | solution.py:280
  9.7 0.0 collective-permute-done.base_ref
  9.7 0.6 %plus.4.base_ref = bf16[14,128,128]{2,1,0:T(8,128)(2,1)S(1)} custom-call(f32[8]{0:T(128)S(1)} %get-tuple-element.60.flag_ref, bf16[14,128,128]{2,1,0:T(8,128)(2,1)S(1)} %collective-permute-done.base_ref, bf16[14,128,128]{2,1,0:T(8,128)(2,1)S(1)} %get-tuple-element.62.x_ref.keep_ref), custom_call_target="tpu_custom_call" | custom-call | flops 1024 | bytes 1024 | tf_op jit(solution)/shard_map/plus/pallas_call | solution.py:283
  10.4 1.3 %collective-permute-start.1 = (bf16[14,128,128]{2,1,0:T(8,128)(2,1)S(1)}, bf16[14,128,128]{2,1,0:T(8,128)(2,1)S(1)}, u32[]{:S(2)}, u32[]{:S(2)}) collective-permute-start(bf16[14,128,128]{2,1,0:T(8,128)(2,1)S(1)} %plus.4.base_ref), channel_id=1, source_target_pairs={{0,4},{2,6},{4,8},{5,1},{6,10},{7,3},{8,12},{9,5},{10,14},{11,7},{... | collective-permute-start | bytes 1376264 | tf_op jit(solution)/shard_map/ppermute | solution.py:280
  11.7 6.2 %local.3 = (bf16[192,1792]{1,0:T(8,128)(2,1)S(1)}, bf16[192,1792]{1,0:T(8,128)(2,1)S(1)}, bf16[192,1792]{1,0:T(8,128)(2,1)S(1)}, bf16[192,1792]{1,0:T(8,128)(2,1)S(1)}) custom-call(s32[1]{0:T(128)} %bitcast.pos_ref.refs_0_, s32[4]{0:T(128)S(1)} %copy-done, bf16[192,4096]{1,0:T(8,128)(2,1)S(1)} %get-tuple-element.85.q_ref.refs_2_, ...), custom_call_target="tpu_custom_call" | custom-call | flops 1024 | bytes 1024 | tf_op jit(solution)/shard_map/local/pallas_call | solution.py:244
  17.9 8.2 %collective-permute-done.1.x_ref.far_ref = bf16[14,128,128]{2,1,0:T(8,128)(2,1)S(1)} collective-permute-done((bf16[14,128,128]{2,1,0:T(8,128)(2,1)S(1)}, bf16[14,128,128]{2,1,0:T(8,128)(2,1)S(1)}, u32[]{:S(2)}, u32[]{:S(2)}) %collective-permute-start.1) | collective-permute-done | bytes 458784 | tf_op jit(solution)/shard_map/ppermute | solution.py:280
  26.1 0.6 %plus.5 = bf16[14,128,128]{2,1,0:T(8,128)(2,1)S(1)} custom-call(f32[8]{0:T(128)S(1)} %get-tuple-element.60.flag_ref, bf16[14,128,128]{2,1,0:T(8,128)(2,1)S(1)} %plus.4.base_ref, bf16[14,128,128]{2,1,0:T(8,128)(2,1)S(1)} %collective-permute-done.1.x_ref.far_ref), custom_call_target="tpu_custom_call" | custom-call | flops 1024 | bytes 1024 | tf_op jit(solution)/shard_map/plus/pallas_call | solution.py:283
  26.7 1.3 %collective-permute-start.2 = (bf16[14,128,128]{2,1,0:T(8,128)(2,1)S(1)}, bf16[14,128,128]{2,1,0:T(8,128)(2,1)S(1)}, u32[]{:S(2)}, u32[]{:S(2)}) collective-permute-start(bf16[14,128,128]{2,1,0:T(8,128)(2,1)S(1)} %plus.5), channel_id=1, source_target_pairs={{0,2},{2,4},{3,1},{4,6},{5,3},{6,8},{7,5},{8,10},{9,7},{10,12},{11... | collective-permute-start | bytes 1376264 | tf_op jit(solution)/shard_map/ppermute | solution.py:280
  28.0 2.2 %local.4 = (bf16[192,512]{1,0:T(8,128)(2,1)S(1)}, bf16[192,512]{1,0:T(8,128)(2,1)S(1)}, bf16[192,512]{1,0:T(8,128)(2,1)S(1)}, bf16[192,512]{1,0:T(8,128)(2,1)S(1)}) custom-call(s32[1]{0:T(128)} %bitcast.pos_ref.refs_0_, s32[4]{0:T(128)S(1)} %copy-done, bf16[192,4096]{1,0:T(8,128)(2,1)S(1)} %get-tuple-element.85.q_ref.refs_2_, ...), custom_call_target="tpu_custom_call" | custom-call | flops 1024 | bytes 1024 | tf_op jit(solution)/shard_map/local/pallas_call | solution.py:244
  30.2 0.0 collective-permute-done.5.x_ref.near_ref
  30.2 0.7 %plus.7 = bf16[18,128,128]{2,1,0:T(8,128)(2,1)S(1)} custom-call(f32[8]{0:T(128)S(1)} %get-tuple-element.60.flag_ref, bf16[18,128,128]{2,1,0:T(8,128)(2,1)S(1)} %plus.6.base_ref, bf16[18,128,128]{2,1,0:T(8,128)(2,1)S(1)} %collective-permute-done.5.x_ref.near_ref), custom_call_target="tpu_custom_call" | custom-call | flops 1024 | bytes 1024 | tf_op jit(solution)/shard_map/plus/pallas_call | solution.py:283
  30.9 1.3 %collective-permute-start.6 = (bf16[18,128,128]{2,1,0:T(8,128)(2,1)S(1)}, bf16[18,128,128]{2,1,0:T(8,128)(2,1)S(1)}, u32[]{:S(2)}, u32[]{:S(2)}) collective-permute-start(bf16[18,128,128]{2,1,0:T(8,128)(2,1)S(1)} %plus.7), channel_id=1, source_target_pairs={{0,4},{2,6},{4,8},{5,1},{6,10},{7,3},{8,12},{9,5},{10,14},{11,7},{... | collective-permute-start | bytes 1769480 | tf_op jit(solution)/shard_map/ppermute | solution.py:280
  32.2 6.2 %local.5 = (bf16[192,1792]{1,0:T(8,128)(2,1)S(1)}, bf16[192,1792]{1,0:T(8,128)(2,1)S(1)}, bf16[192,1792]{1,0:T(8,128)(2,1)S(1)}, bf16[192,1792]{1,0:T(8,128)(2,1)S(1)}) custom-call(s32[1]{0:T(128)} %bitcast.pos_ref.refs_0_, s32[4]{0:T(128)S(1)} %copy-done, bf16[192,4096]{1,0:T(8,128)(2,1)S(1)} %get-tuple-element.85.q_ref.refs_2_, ...), custom_call_target="tpu_custom_call" | custom-call | flops 10000000000 | bytes 1024 | tf_op jit(solution)/shard_map/local/pallas_call | solution.py:244
  38.5 3.7 %collective-permute-done.6.far_ref = bf16[18,128,128]{2,1,0:T(8,128)(2,1)S(1)} collective-permute-done((bf16[18,128,128]{2,1,0:T(8,128)(2,1)S(1)}, bf16[18,128,128]{2,1,0:T(8,128)(2,1)S(1)}, u32[]{:S(2)}, u32[]{:S(2)}) %collective-permute-start.6) | collective-permute-done | bytes 589856 | tf_op jit(solution)/shard_map/ppermute | solution.py:280
  42.2 0.7 %close.3 = (bf16[18,128,128]{2,1,0:T(8,128)(2,1)S(1)}, bf16[18,128,128]{2,1,0:T(8,128)(2,1)S(1)}) custom-call(f32[8]{0:T(128)S(1)} %get-tuple-element.60.flag_ref, bf16[18,128,128]{2,1,0:T(8,128)(2,1)S(1)} %collective-permute-done.5.x_ref.near_ref, bf16[18,128,128]{2,1,0:T(8,128)(2,1)S(1)} %collective-permute-done.6.far_ref, ...), custom_call_target="tpu_custom_call" | custom-call | flops 1024 | bytes 1024 | tf_op jit(solution)/shard_map/close/pallas_call | solution.py:294
  42.9 2.3 %collective-permute-start.7 = (bf16[18,128,128]{2,1,0:T(8,128)(2,1)S(1)}, bf16[18,128,128]{2,1,0:T(8,128)(2,1)S(1)}, u32[]{:S(2)}, u32[]{:S(2)}) collective-permute-start(bf16[18,128,128]{2,1,0:T(8,128)(2,1)S(1)} %get-tuple-element.95), channel_id=1, source_target_pairs={{0,1},{1,0},{2,3},{3,2},{4,5},{5,4},{6,7},{7,6},{8,9},{9,8},{10,11... | collective-permute-start | bytes 1769480 | tf_op jit(solution)/shard_map/ppermute | solution.py:276
  45.3 0.0 collective-permute-done.2.near_ref
  45.3 0.7 %close.2 = (bf16[14,128,128]{2,1,0:T(8,128)(2,1)S(1)}, bf16[14,128,128]{2,1,0:T(8,128)(2,1)S(1)}) custom-call(f32[8]{0:T(128)S(1)} %get-tuple-element.60.flag_ref, bf16[14,128,128]{2,1,0:T(8,128)(2,1)S(1)} %collective-permute-done.2.near_ref, bf16[14,128,128]{2,1,0:T(8,128)(2,1)S(1)} %collective-permute-done.1.x_ref.far_ref, ...), custom_call_target="tpu_custom_call" | custom-call | flops 1024 | bytes 1024 | tf_op jit(solution)/shard_map/close/pallas_call | solution.py:294
  46.0 0.1 collective-permute-start.3
  46.1 0.8 %collective-permute-done.7.refs_7_ = bf16[18,128,128]{2,1,0:T(8,128)(2,1)S(1)} collective-permute-done((bf16[18,128,128]{2,1,0:T(8,128)(2,1)S(1)}, bf16[18,128,128]{2,1,0:T(8,128)(2,1)S(1)}, u32[]{:S(2)}, u32[]{:S(2)}) %collective-permute-start.7) | collective-permute-done | bytes 589856 | tf_op jit(solution)/shard_map/ppermute | solution.py:276
  46.9 3.6 %final.2 = (bf16[192,4096]{1,0:T(8,128)(2,1)}, bf16[192,4096]{1,0:T(8,128)(2,1)}, bf16[192,4096]{1,0:T(8,128)(2,1)}, bf16[192,4096]{1,0:T(8,128)(2,1)}) custom-call(s32[1]{0:T(128)} %bitcast.pos_ref.refs_0_, s32[4]{0:T(128)S(1)} %copy-done, bf16[192,4096]{1,0:T(8,128)(2,1)S(1)} %get-tuple-element.85.q_ref.refs_2_, ...), custom_call_target="tpu_custom_call" | custom-call | flops 1024 | bytes 1024 | tf_op jit(solution)/shard_map/final/pallas_call | solution.py:263
  50.5 0.0 collective-permute-done.3.refs_7_
  50.5 3.2 %final.3 = (bf16[192,4096]{1,0:T(8,128)(2,1)}, bf16[192,4096]{1,0:T(8,128)(2,1)}, bf16[192,4096]{1,0:T(8,128)(2,1)}, bf16[192,4096]{1,0:T(8,128)(2,1)}) custom-call(s32[1]{0:T(128)} %bitcast.pos_ref.refs_0_, s32[4]{0:T(128)S(1)} %copy-done, ...), custom_call_target="tpu_custom_call", output_to_operand_aliasing={{0}: (12, {}), {1}: (13, {}), {2}: (14, {}), {3}: (15, {})} | custom-call | flops 1024 | bytes 1024 | tf_op jit(solution)/shard_map/final/pallas_call | solution.py:263
Async XLA Ops:
  0.6 0.7 %copy-start = (s32[4]{0:T(128)S(1)}, s32[4]{0:T(128)}, u32[]{:S(2)}) copy-start(s32[4]{0:T(128)} %refs_1_.3) | copy-start | bytes 52
  5.7 2.1 %collective-permute-start.4 = (bf16[18,128,128]{2,1,0:T(8,128)(2,1)S(1)}, bf16[18,128,128]{2,1,0:T(8,128)(2,1)S(1)}, u32[]{:S(2)}, u32[]{:S(2)}) collective-permute-start(bf16[18,128,128]{2,1,0:T(8,128)(2,1)S(1)} %get-tuple-element.74), channel_id=1, source_target_pairs={{0,1},{1,0},{2,3},{3,2},{4,5},{5,4},{6,7},{7,6},{8,9},{9,8},{10,11... | collective-permute-start | bytes 1769480 | tf_op jit(solution)/shard_map/ppermute | solution.py:276
  7.1 2.7 %collective-permute-start = (bf16[14,128,128]{2,1,0:T(8,128)(2,1)S(1)}, bf16[14,128,128]{2,1,0:T(8,128)(2,1)S(1)}, u32[]{:S(2)}, u32[]{:S(2)}) collective-permute-start(bf16[14,128,128]{2,1,0:T(8,128)(2,1)S(1)} %get-tuple-element.61), channel_id=1, source_target_pairs={{0,1},{1,0},{2,3},{3,2},{4,5},{5,4},{6,7},{7,6},{8,9},{9,8},{10,11... | collective-permute-start | bytes 1376264 | tf_op jit(solution)/shard_map/ppermute | solution.py:276
  8.4 21.8 %collective-permute-start.5 = (bf16[18,128,128]{2,1,0:T(8,128)(2,1)S(1)}, bf16[18,128,128]{2,1,0:T(8,128)(2,1)S(1)}, u32[]{:S(2)}, u32[]{:S(2)}) collective-permute-start(bf16[18,128,128]{2,1,0:T(8,128)(2,1)S(1)} %plus.6.base_ref), channel_id=1, source_target_pairs={{0,2},{2,4},{3,1},{4,6},{5,3},{6,8},{7,5},{8,10},{9,7},{10,12},{11... | collective-permute-start | bytes 1769480 | tf_op jit(solution)/shard_map/ppermute | solution.py:280
  10.4 15.7 %collective-permute-start.1 = (bf16[14,128,128]{2,1,0:T(8,128)(2,1)S(1)}, bf16[14,128,128]{2,1,0:T(8,128)(2,1)S(1)}, u32[]{:S(2)}, u32[]{:S(2)}) collective-permute-start(bf16[14,128,128]{2,1,0:T(8,128)(2,1)S(1)} %plus.4.base_ref), channel_id=1, source_target_pairs={{0,4},{2,6},{4,8},{5,1},{6,10},{7,3},{8,12},{9,5},{10,14},{11,7},{... | collective-permute-start | bytes 1376264 | tf_op jit(solution)/shard_map/ppermute | solution.py:280
  26.7 18.5 %collective-permute-start.2 = (bf16[14,128,128]{2,1,0:T(8,128)(2,1)S(1)}, bf16[14,128,128]{2,1,0:T(8,128)(2,1)S(1)}, u32[]{:S(2)}, u32[]{:S(2)}) collective-permute-start(bf16[14,128,128]{2,1,0:T(8,128)(2,1)S(1)} %plus.5), channel_id=1, source_target_pairs={{0,2},{2,4},{3,1},{4,6},{5,3},{6,8},{7,5},{8,10},{9,7},{10,12},{11... | collective-permute-start | bytes 1376264 | tf_op jit(solution)/shard_map/ppermute | solution.py:280
  30.9 11.2 %collective-permute-start.6 = (bf16[18,128,128]{2,1,0:T(8,128)(2,1)S(1)}, bf16[18,128,128]{2,1,0:T(8,128)(2,1)S(1)}, u32[]{:S(2)}, u32[]{:S(2)}) collective-permute-start(bf16[18,128,128]{2,1,0:T(8,128)(2,1)S(1)} %plus.7), channel_id=1, source_target_pairs={{0,4},{2,6},{4,8},{5,1},{6,10},{7,3},{8,12},{9,5},{10,14},{11,7},{... | collective-permute-start | bytes 1769480 | tf_op jit(solution)/shard_map/ppermute | solution.py:280
  42.9 4.0 %collective-permute-start.7 = (bf16[18,128,128]{2,1,0:T(8,128)(2,1)S(1)}, bf16[18,128,128]{2,1,0:T(8,128)(2,1)S(1)}, u32[]{:S(2)}, u32[]{:S(2)}) collective-permute-start(bf16[18,128,128]{2,1,0:T(8,128)(2,1)S(1)} %get-tuple-element.95), channel_id=1, source_target_pairs={{0,1},{1,0},{2,3},{3,2},{4,5},{5,4},{6,7},{7,6},{8,9},{9,8},{10,11... | collective-permute-start | bytes 1769480 | tf_op jit(solution)/shard_map/ppermute | solution.py:276
  46.0 4.5 %collective-permute-start.3 = (bf16[14,128,128]{2,1,0:T(8,128)(2,1)S(1)}, bf16[14,128,128]{2,1,0:T(8,128)(2,1)S(1)}, u32[]{:S(2)}, u32[]{:S(2)}) collective-permute-start(bf16[14,128,128]{2,1,0:T(8,128)(2,1)S(1)} %get-tuple-element.69), channel_id=1, source_target_pairs={{0,1},{1,0},{2,3},{3,2},{4,5},{5,4},{6,7},{7,6},{8,9},{9,8},{10,11... | collective-permute-start | bytes 1376264 | tf_op jit(solution)/shard_map/ppermute | solution.py:276

commit v3 on v2

v3 whole, which is shorter than its diff:
```python
import functools
import math

import jax
import jax.numpy as jnp
from jax import lax
from jax.experimental import pallas as pl
from jax.experimental.pallas import tpu as pltpu
from jax.sharding import PartitionSpec as P

DH = 128
UNIT = 128
LONGEST = 10
N_X = 18
EVEN = 5
F32 = jnp.float32
BF16 = jnp.bfloat16


def doc_of(pos, doc_ref, docs):
    count = jnp.int32(0)
    end = jnp.int32(0)
    for d in range(docs):
        end = end + doc_ref[d] * UNIT
        count = count + (pos >= end).astype(jnp.int32)
    return jnp.where(pos < 0, jnp.int32(-1), count)


def edges(pos_ref, doc_ref, rows, docs):
    first = pos_ref[0] * rows
    start = jnp.int32(0)
    stop = jnp.int32(1 << 30)
    end = jnp.int32(0)
    for d in range(docs):
        end = end + doc_ref[d] * UNIT
        start = jnp.where(end <= first + (rows - 1), end, start)
        stop = jnp.minimum(stop, jnp.where(end > first, end, jnp.int32(1 << 30)))
    return start - first, stop - first


def dot_tt(a, b):
    return lax.dot_general(a, b, (((0,), (0,)), ((), ())), preferred_element_type=F32)


def dot_nt(a, b):
    return lax.dot_general(a, b, (((1,), (1,)), ((), ())), preferred_element_type=F32)


def dot_nn(a, b):
    return lax.dot_general(a, b, (((1,), (0,)), ((), ())), preferred_element_type=F32)


def tails_of(q_ref, k_ref, v_ref, g_ref, flag_ref, rows_ref, keep_ref, send_ref, lo, sizes, ready=None):
    even = jnp.broadcast_to(flag_ref[EVEN : EVEN + 1, :], (DH, DH)) > 0
    at = 0
    for c, size in enumerate(sizes):
        if ready is not None:
            ready(c)
        for i in range(at, at + size):
            cols = pl.ds((lo + i) * DH, DH)
            tail = dot_tt(k_ref[:, cols] * rows_ref[0], v_ref[:, cols])
            head = dot_tt(q_ref[:, cols] * rows_ref[1], g_ref[:, cols])
            keep_ref[i] = jnp.where(even, tail, head).astype(BF16)
            send_ref[i] = jnp.where(even, head, tail).astype(BF16)
        at += size


def open_kernel(dev_ref, doc_hbm, q_hbm, k_hbm, v_hbm, g_hbm, q_ref, k_ref, v_ref, g_ref, keep_ref, send_ref, flag_ref, rows_ref, reach_ref, allowed_ref, doc_ref, doc_sem, sems, *, docs, sizes, scale):
    rows, width = q_ref.shape
    arrays = ((k_hbm, k_ref), (v_hbm, v_ref), (q_hbm, q_ref), (g_hbm, g_ref))
    rest = width // DH - sum(sizes)
    bounds = pltpu.make_async_copy(doc_hbm, doc_ref, doc_sem)
    bounds.start()
    copies = []
    at = 0
    for c, size in enumerate((*sizes, rest)):
        cols = pl.ds(at * DH, size * DH)
        group = [pltpu.make_async_copy(src.at[:, cols], dst.at[:, cols], sems.at[c, a]) for a, (src, dst) in enumerate(arrays)]
        for cp in group:
            cp.start()
        copies.append(group)
        at += size
    bounds.wait()
    dev = dev_ref[0]
    core = lax.rem(dev, 2)
    chip = dev - core
    first = dev * rows

    def key(u):
        pos = jnp.where(core == 0, rows * (chip + 2 - u) - 1, rows * (chip + u))
        return doc_of(pos, doc_ref, docs)

    k0, k1, k2, k4 = key(0), key(1), key(2), key(4)
    row = lax.broadcasted_iota(jnp.int32, (8, DH), 0)
    flags = jnp.zeros((8, DH), F32)
    for i, flag in enumerate((k1 == k0, k2 == k0, k4 == k2, k4 == k0, k2 == k1, core == 0)):
        flags = flags + jnp.where(row == i, flag.astype(F32), 0.0)
    flag_ref[...] = flags
    start, stop = edges(dev_ref, doc_ref, rows, docs)
    into = jnp.where(doc_of(first, doc_ref, docs) == doc_of(first - 1, doc_ref, docs), stop, 0)
    onto = jnp.where(doc_of(first + (rows - 1), doc_ref, docs) == doc_of(first + rows, doc_ref, docs), start, rows)
    row = lax.broadcasted_iota(jnp.int32, (rows, DH), 0)
    rows_ref[0] = jnp.where(row >= start, 1.0, 0.0).astype(BF16)
    rows_ref[1] = jnp.where(row < stop, 1.0, 0.0).astype(BF16)
    reach_ref[0] = jnp.where(row < into, scale, 0.0)
    reach_ref[1] = jnp.where(row >= onto, scale, 0.0)
    t = lax.broadcasted_iota(jnp.int32, (rows, rows), 0)
    s = lax.broadcasted_iota(jnp.int32, (rows, rows), 1)
    allowed_ref[...] = jnp.where((s <= t) & ((t < start) | (s >= start)), 1.0, 0.0).astype(BF16)

    def ready(c):
        for cp in copies[c]:
            cp.wait()

    tails_of(q_ref, k_ref, v_ref, g_ref, flag_ref, rows_ref, keep_ref, send_ref, 0, sizes, ready)
    ready(len(sizes))


def tails_kernel(q_ref, k_ref, v_ref, g_ref, flag_ref, rows_ref, keep_ref, send_ref, *, lo, n):
    tails_of(q_ref, k_ref, v_ref, g_ref, flag_ref, rows_ref, keep_ref, send_ref, lo, (n,))


def local_kernel(q_ref, k_ref, v_ref, g_ref, allowed_ref, o_ref, dq_ref, dk_ref, dv_ref, *, lo, n, scale, unroll):
    def step(j, carry):
        for u in range(unroll):
            i = j * unroll + u
            src = pl.ds(pl.multiple_of((lo + i) * DH, DH), DH)
            dst = pl.ds(pl.multiple_of(i * DH, DH), DH)
            q, k, v, g = q_ref[:, src], k_ref[:, src], v_ref[:, src], g_ref[:, src]
            probs = dot_nt(q, k).astype(BF16) * allowed_ref[...]
            dprobs = dot_nt(g, v).astype(BF16) * allowed_ref[...]
            o_ref[:, dst] = (scale * dot_nn(probs, v)).astype(BF16)
            dq_ref[:, dst] = (scale * dot_nn(dprobs, k)).astype(BF16)
            dk_ref[:, dst] = (scale * dot_tt(dprobs, q)).astype(BF16)
            dv_ref[:, dst] = (scale * dot_tt(probs, g)).astype(BF16)
        return carry

    lax.fori_loop(0, n // unroll, step, 0)


def final_kernel(q_ref, k_ref, v_ref, g_ref, flag_ref, reach_ref, mine_ref, other_ref, parts, outs, bufs, sems, *, lo, sizes):
    even = jnp.broadcast_to(flag_ref[EVEN : EVEN + 1, :], (DH, DH)) > 0
    copies = []
    at = 0
    for c, size in enumerate(sizes):
        for i in range(at, at + size):
            cols = pl.ds(i * DH, DH)
            src = pl.ds((lo + i) * DH, DH)
            q, k, v, g = q_ref[:, src], k_ref[:, src], v_ref[:, src], g_ref[:, src]
            mine, other = mine_ref[i].astype(F32), other_ref[i].astype(F32)
            state = jnp.where(even, mine, other).astype(BF16)
            back = jnp.where(even, other, mine).astype(BF16)
            terms = ((0, dot_nn(q, state)), (0, dot_nt(g, state)), (1, dot_nt(v, back)), (1, dot_nn(k, back)))
            for a, (side, term) in enumerate(terms):
                bufs[a][:, cols] = (parts[a][:, cols].astype(F32) + reach_ref[side] * term).astype(BF16)
        for a in range(4):
            cp = pltpu.make_async_copy(
                bufs[a].at[:, pl.ds(at * DH, size * DH)],
                outs[a].at[:, pl.ds((lo + at) * DH, size * DH)],
                sems.at[c, a],
            )
            cp.start()
            copies.append(cp)
        at += size
    for cp in copies:
        cp.wait()


def flag_of(flag_ref, which):
    return jnp.broadcast_to(flag_ref[which : which + 1, :], (DH, DH)).astype(BF16)


def plus_kernel(flag_ref, base_ref, x_ref, out_ref, *, which):
    flag = flag_of(flag_ref, which)
    for i in range(base_ref.shape[0]):
        out_ref[i] = base_ref[i] + flag * x_ref[i]


def close_kernel(flag_ref, near_ref, far_ref, keep_ref, mine_ref, pass_ref):
    flag, flag2 = flag_of(flag_ref, 2), flag_of(flag_ref, 4)
    for i in range(near_ref.shape[0]):
        mine = near_ref[i] + flag * far_ref[i]
        mine_ref[i] = mine
        pass_ref[i] = keep_ref[i] + flag2 * mine


def split(n, size):
    return (size,) * (n // size) + ((n % size,) if n % size else ())


def on_device(queries, keys, values, out_grad, doc_blocks):
    rows, width = queries.shape
    n_heads = width // DH
    docs = doc_blocks.shape[0]
    devices = lax.axis_size("seq")
    scale = 1.0 / math.sqrt(DH * n_heads * LONGEST)
    dev = lax.axis_index("seq").astype(jnp.int32).reshape(1)
    smem = pl.BlockSpec(memory_space=pltpu.SMEM)
    vmem = pl.BlockSpec(memory_space=pltpu.VMEM)
    hbm = pl.BlockSpec(memory_space=pltpu.HBM)
    params = pltpu.CompilerParams(vmem_limit_bytes=24 << 20)

    def shaped(*shape):
        return jax.ShapeDtypeStruct(shape, BF16)

    def call(body, ins, outs, name, flops=1024, **kw):
        return pl.pallas_call(
            body,
            in_specs=[vmem] * len(ins),
            out_specs=[vmem] * len(outs),
            out_shape=outs,
            compiler_params=params,
            cost_estimate=pl.CostEstimate(flops=flops, transcendentals=0, bytes_accessed=1024),
            name=name,
        )(*ins)

    def opened(n):
        sizes = split(n, 4)
        out = pl.pallas_call(
            functools.partial(open_kernel, docs=docs, sizes=sizes, scale=scale),
            in_specs=[smem] + [hbm] * 5,
            out_specs=[vmem] * 10,
            out_shape=[shaped(rows, width)] * 4
            + [shaped(n, DH, DH)] * 2
            + [jax.ShapeDtypeStruct((8, DH), F32), shaped(2, rows, DH), jax.ShapeDtypeStruct((2, rows, DH), F32), shaped(rows, rows)],
            scratch_shapes=[pltpu.SMEM((docs,), jnp.int32), pltpu.SemaphoreType.DMA, pltpu.SemaphoreType.DMA((len(sizes) + 1, 4))],
            compiler_params=params,
            cost_estimate=pl.CostEstimate(flops=1000, transcendentals=0, bytes_accessed=1024),
            name="opened",
        )(dev, *(pltpu.with_memory_space_constraint(x, pltpu.HBM) for x in (doc_blocks, queries, keys, values, out_grad)))
        return out[:4], out[4], out[5], out[6:]

    def tails(lo, n):
        body = functools.partial(tails_kernel, lo=lo, n=n)
        return call(body, (*blocks, flags, edge_rows), [shaped(n, DH, DH)] * 2, "tails", 1000000000)

    def local(blocks, lo, n, flops):
        body = functools.partial(local_kernel, lo=lo, n=n, scale=scale, unroll=2)
        return call(body, (*blocks, allowed), [shaped(rows, n * DH)] * 4, "local", flops)

    def final(lo, n, mine, other, parts, outs):
        aliased = [] if outs is None else list(outs)
        sizes = split(n, 4)

        def body(*refs):
            ins, rest = refs[:12], refs[12 + len(aliased) :]
            final_kernel(*ins[:8], ins[8:], rest[:4], rest[4:8], rest[8], lo=lo, sizes=sizes)

        return pl.pallas_call(
            body,
            in_specs=[vmem] * 12 + [hbm] * len(aliased),
            out_specs=[hbm] * 4,
            out_shape=[shaped(rows, width)] * 4,
            scratch_shapes=[pltpu.VMEM((rows, n * DH), BF16)] * 4 + [pltpu.SemaphoreType.DMA((len(sizes), 4))],
            input_output_aliases={12 + i: i for i in range(len(aliased))},
            compiler_params=params,
            cost_estimate=pl.CostEstimate(flops=1000000000, transcendentals=0, bytes_accessed=1024),
            name="final",
        )(*blocks, flags, reach, mine, other, *parts, *aliased)

    def across(x):
        return lax.ppermute(x, "seq", [(i, i ^ 1) for i in range(devices)])

    def along(x, by):
        pairs = [(i, i + by if i % 2 == 0 else i - by) for i in range(devices)]
        return lax.ppermute(x, "seq", [(i, j) for i, j in pairs if 0 <= j < devices])

    def plus(base, which, x):
        return call(functools.partial(plus_kernel, which=which), (flags, base, x), [shaped(*base.shape)], "plus", 1000000000)[0]

    def close(near, far, keep):
        return call(close_kernel, (flags, near, far, keep), [shaped(*near.shape)] * 2, "close", 10000000000)

    n_w = n_heads - N_X
    blocks, keep_x, send_x, (flags, edge_rows, reach, allowed) = opened(N_X)
    keep_w, send_w = tails(N_X, n_w)
    total_x = plus(across(send_x), 0, keep_x)
    total_w = plus(across(send_w), 0, keep_w)
    near_x = along(total_x, 2)
    far_w = along(total_w, 4)
    part_w = local(blocks, N_X, n_w, 1000000000)
    far_w, part_w = lax.optimization_barrier((far_w, part_w))
    gathered_w = plus(total_w, 3, far_w)
    near_w = along(gathered_w, 2)
    near_x, _ = lax.optimization_barrier((near_x, gathered_w))
    gathered_x = plus(total_x, 1, near_x)
    far_x = along(gathered_x, 4)
    later, _ = lax.optimization_barrier((blocks, gathered_x))
    part_x = local(later, 0, N_X, 10000000000)
    far_x, part_x = lax.optimization_barrier((far_x, part_x))
    mine_x, pass_x = close(near_x, far_x, keep_x)
    other_x = across(pass_x)
    outs = final(0, N_X, mine_x, other_x, part_x, None)
    near_w, _ = lax.optimization_barrier((near_w, pass_x))
    mine_w, pass_w = close(near_w, far_w, keep_w)
    other_w = across(pass_w)
    outs = final(N_X, n_w, mine_w, other_w, part_w, outs)
    return tuple(outs)


def solution(mesh):
    spec = P(("sweep", "seq"), None)
    return jax.shard_map(
        on_device,
        mesh=mesh,
        in_specs=(spec, spec, spec, spec, P("sweep")),
        out_specs=(spec, spec, spec, spec),
        check_vma=False,
    )
```

time: 54.2 us -> 47 us (0.87)
  Pallas kernels: 31.2 us -> 23 us
  waiting for transfers between devices: 12.8 us -> 16.4 us
  starting transfers between devices: 8.24 us -> 6.43 us
  local copies, waits for them, and re-layouts: 0.65 us -> 0 us
    pallas_call x13 -> x12, Pallas kernels: 31.2 us -> 23 us  [the longest x9 14.8 us: call(): pl.pallas_call(body, in_specs=[vmem] * len(ins), out_specs=[vmem] * len(o...]
    ppermute x4, waiting for transfers between devices: 11.9 us -> 14.5 us  [along(): lax.ppermute(x, 'seq', [(i, j) for i, j in pairs if 0 <= j < devices])]
    ppermute x4, starting transfers between devices: 3.07 us -> 1.26 us  [across(): return lax.ppermute(x, 'seq', [(i, i ^ 1) for i in range(devices)])]
    ppermute x4, waiting for transfers between devices: 0.89 us -> 1.88 us  [across(): return lax.ppermute(x, 'seq', [(i, i ^ 1) for i in range(devices)])]
    unnamed x2 -> x0, local copies, waits for them, and re-layouts: 0.65 us -> none
  transfers between devices with their start and end apart: 8 -> 8, of which waited for: 4 -> 4; matrix products, arithmetic and copies ran while one was open for 0% -> 0% of each run, Pallas kernels for 44% -> 37%
where the time goes in v3:
time: 47 us; the launch traced here: 46.6 us
  Pallas kernels  23 us (49%)
  waiting for transfers between devices  16.4 us (35%)
  starting transfers between devices  6.43 us (14%)
  between operations  0.78 us (2%)
    pallas_call x9, Pallas kernels, call(): pl.pallas_call(body, in_specs=[vmem] * len(ins), out_specs=[vmem] * len(o...  14.8 us
    ppermute x4, waiting for transfers between devices, along(): lax.ppermute(x, 'seq', [(i, j) for i, j in pairs if 0 <= j < devices])  14.5 us
    ppermute x4, starting transfers between devices, along(): lax.ppermute(x, 'seq', [(i, j) for i, j in pairs if 0 <= j < devices])  5.17 us
    pallas_call x2, Pallas kernels, final(): pl.pallas_call(body, in_specs=[vmem] * 12 + [hbm] * len(aliased), out_spe...  5.04 us
    pallas_call x1, Pallas kernels, opened(): pl.pallas_call(functools.partial(open_kernel, docs=docs, sizes=sizes, sca...  3.22 us
    ppermute x4, waiting for transfers between devices, across(): return lax.ppermute(x, 'seq', [(i, i ^ 1) for i in range(devices)])  1.88 us
    ppermute x4, starting transfers between devices, across(): return lax.ppermute(x, 'seq', [(i, i ^ 1) for i in range(devices)])  1.26 us
  transfers between devices with their start and end apart: 8, of which 4 were waited for; matrix products, arithmetic and copies ran while one was open for 0% of the time, Pallas kernels for 37%

profile of v3, /device:TPU:1, one launch (start us, length us, event | category | flops | bytes accessed | tf_op | source)
XLA Modules:
  0.0 46.6 jit_solution(18010111113165374275)
XLA Ops:
  0.6 3.2 %opened.1 = (bf16[192,4096]{1,0:T(8,128)(2,1)S(1)}, bf16[192,4096]{1,0:T(8,128)(2,1)S(1)}, bf16[192,4096]{1,0:T(8,128)(2,1)S(1)}, bf16[192,4096]{1,0:T(8,128)(2,...) custom-call(s32[1]{0:T(128)} %bitcast.dev_ref, ...), custom_call_target="tpu_custom_call" | custom-call | flops 1000 | bytes 1024 | tf_op jit(solution)/shard_map/opened/pallas_call | solution.py:219
  3.9 0.1 collective-permute-start.3
  3.9 0.8 %tails.1 = (bf16[14,128,128]{2,1,0:T(8,128)(2,1)S(1)}, bf16[14,128,128]{2,1,0:T(8,128)(2,1)S(1)}) custom-call(bf16[192,4096]{1,0:T(8,128)(2,1)S(1)} %get-tuple-element.66.q_ref.refs_0_, bf16[192,4096]{1,0:T(8,128)(2,1)S(1)} %get-tuple-element.67.k_ref.refs_1_, bf16[192,4096]{1,0:T(8,128)(2,1)S(1)} %get-tuple-element.68.v_ref.refs_2_, ...), custom_call_target="tpu_custom_call" | custom-call | flops 1000000000 | bytes 1024 | tf_op jit(solution)/shard_map/tails/pallas_call | solution.py:207
  4.7 0.6 %collective-permute-start = (bf16[14,128,128]{2,1,0:T(8,128)(2,1)S(1)}, bf16[14,128,128]{2,1,0:T(8,128)(2,1)S(1)}, u32[]{:S(2)}, u32[]{:S(2)}) collective-permute-start(bf16[14,128,128]{2,1,0:T(8,128)(2,1)S(1)} %get-tuple-element.55), channel_id=1, source_target_pairs={{0,1},{1,0},{2,3},{3,2},{4,5},{5,4},{6,7},{7,6},{8,9},{9,8},{10,11... | collective-permute-start | bytes 1376264 | tf_op jit(solution)/shard_map/ppermute | solution.py:262
  5.3 0.7 %collective-permute-done.3.base_ref = bf16[18,128,128]{2,1,0:T(8,128)(2,1)S(1)} collective-permute-done((bf16[18,128,128]{2,1,0:T(8,128)(2,1)S(1)}, bf16[18,128,128]{2,1,0:T(8,128)(2,1)S(1)}, u32[]{:S(2)}, u32[]{:S(2)}) %collective-permute-start.3) | collective-permute-done | bytes 589856 | tf_op jit(solution)/shard_map/ppermute | solution.py:262
  5.9 0.1 plus.6.base_ref
  6.1 1.3 %collective-permute-start.4 = (bf16[18,128,128]{2,1,0:T(8,128)(2,1)S(1)}, bf16[18,128,128]{2,1,0:T(8,128)(2,1)S(1)}, u32[]{:S(2)}, u32[]{:S(2)}) collective-permute-start(bf16[18,128,128]{2,1,0:T(8,128)(2,1)S(1)} %plus.6.base_ref), channel_id=1, source_target_pairs={{0,2},{2,4},{3,1},{4,6},{5,3},{6,8},{7,5},{8,10},{9,7},{10,12},{11... | collective-permute-start | bytes 1769480 | tf_op jit(solution)/shard_map/ppermute | solution.py:266
  7.4 0.0 collective-permute-done.base_ref
  7.4 0.1 plus.4.base_ref
  7.5 1.3 %collective-permute-start.1 = (bf16[14,128,128]{2,1,0:T(8,128)(2,1)S(1)}, bf16[14,128,128]{2,1,0:T(8,128)(2,1)S(1)}, u32[]{:S(2)}, u32[]{:S(2)}) collective-permute-start(bf16[14,128,128]{2,1,0:T(8,128)(2,1)S(1)} %plus.4.base_ref), channel_id=1, source_target_pairs={{0,4},{2,6},{4,8},{5,1},{6,10},{7,3},{8,12},{9,5},{10,14},{11,7},{... | collective-permute-start | bytes 1376264 | tf_op jit(solution)/shard_map/ppermute | solution.py:266
  8.8 5.7 %local.2 = (bf16[192,1792]{1,0:T(8,128)(2,1)S(1)}, bf16[192,1792]{1,0:T(8,128)(2,1)S(1)}, bf16[192,1792]{1,0:T(8,128)(2,1)S(1)}, bf16[192,1792]{1,0:T(8,128)(2,1)S(1)}) custom-call(bf16[192,4096]{1,0:T(8,128)(2,1)S(1)} %get-tuple-element.66.q_ref.refs_0_, bf16[192,4096]{1,0:T(8,128)(2,1)S(1)} %get-tuple-element.67.k_ref.refs_1_, ...), custom_call_target="tpu_custom_call" | custom-call | flops 1000000000 | bytes 1024 | tf_op jit(solution)/shard_map/local/pallas_call | solution.py:207
  14.5 9.2 %collective-permute-done.1.x_ref.far_ref = bf16[14,128,128]{2,1,0:T(8,128)(2,1)S(1)} collective-permute-done((bf16[14,128,128]{2,1,0:T(8,128)(2,1)S(1)}, bf16[14,128,128]{2,1,0:T(8,128)(2,1)S(1)}, u32[]{:S(2)}, u32[]{:S(2)}) %collective-permute-start.1) | collective-permute-done | bytes 458784 | tf_op jit(solution)/shard_map/ppermute | solution.py:266
  23.7 0.1 plus.5
  23.8 1.3 %collective-permute-start.2 = (bf16[14,128,128]{2,1,0:T(8,128)(2,1)S(1)}, bf16[14,128,128]{2,1,0:T(8,128)(2,1)S(1)}, u32[]{:S(2)}, u32[]{:S(2)}) collective-permute-start(bf16[14,128,128]{2,1,0:T(8,128)(2,1)S(1)} %plus.5), channel_id=1, source_target_pairs={{0,2},{2,4},{3,1},{4,6},{5,3},{6,8},{7,5},{8,10},{9,7},{10,12},{11... | collective-permute-start | bytes 1376264 | tf_op jit(solution)/shard_map/ppermute | solution.py:266
  25.1 0.0 collective-permute-done.4.x_ref.near_ref
  25.1 0.1 plus.7
  25.2 1.3 %collective-permute-start.5 = (bf16[18,128,128]{2,1,0:T(8,128)(2,1)S(1)}, bf16[18,128,128]{2,1,0:T(8,128)(2,1)S(1)}, u32[]{:S(2)}, u32[]{:S(2)}) collective-permute-start(bf16[18,128,128]{2,1,0:T(8,128)(2,1)S(1)} %plus.7), channel_id=1, source_target_pairs={{0,4},{2,6},{4,8},{5,1},{6,10},{7,3},{8,12},{9,5},{10,14},{11,7},{... | collective-permute-start | bytes 1769480 | tf_op jit(solution)/shard_map/ppermute | solution.py:266
  26.6 7.4 %local.3 = (bf16[192,2304]{1,0:T(8,128)(2,1)S(1)}, bf16[192,2304]{1,0:T(8,128)(2,1)S(1)}, bf16[192,2304]{1,0:T(8,128)(2,1)S(1)}, bf16[192,2304]{1,0:T(8,128)(2,1)S(1)}) custom-call(bf16[192,4096]{1,0:T(8,128)(2,1)S(1)} %get-tuple-element.66.q_ref.refs_0_, bf16[192,4096]{1,0:T(8,128)(2,1)S(1)} %get-tuple-element.67.k_ref.refs_1_, ...), custom_call_target="tpu_custom_call" | custom-call | flops 10000000000 | bytes 1024 | tf_op jit(solution)/shard_map/local/pallas_call | solution.py:207
  33.9 5.3 %collective-permute-done.5.far_ref = bf16[18,128,128]{2,1,0:T(8,128)(2,1)S(1)} collective-permute-done((bf16[18,128,128]{2,1,0:T(8,128)(2,1)S(1)}, bf16[18,128,128]{2,1,0:T(8,128)(2,1)S(1)}, u32[]{:S(2)}, u32[]{:S(2)}) %collective-permute-start.5) | collective-permute-done | bytes 589856 | tf_op jit(solution)/shard_map/ppermute | solution.py:266
  39.2 0.2 close.2
  39.5 0.1 collective-permute-start.7
  39.6 0.0 collective-permute-done.2.near_ref
  39.6 0.2 close.3
  39.8 0.6 %collective-permute-start.6 = (bf16[14,128,128]{2,1,0:T(8,128)(2,1)S(1)}, bf16[14,128,128]{2,1,0:T(8,128)(2,1)S(1)}, u32[]{:S(2)}, u32[]{:S(2)}) collective-permute-start(bf16[14,128,128]{2,1,0:T(8,128)(2,1)S(1)} %get-tuple-element.78), channel_id=1, source_target_pairs={{0,1},{1,0},{2,3},{3,2},{4,5},{5,4},{6,7},{7,6},{8,9},{9,8},{10,11... | collective-permute-start | bytes 1376264 | tf_op jit(solution)/shard_map/ppermute | solution.py:262
  40.3 1.2 %collective-permute-done.7.refs_7_ = bf16[18,128,128]{2,1,0:T(8,128)(2,1)S(1)} collective-permute-done((bf16[18,128,128]{2,1,0:T(8,128)(2,1)S(1)}, bf16[18,128,128]{2,1,0:T(8,128)(2,1)S(1)}, u32[]{:S(2)}, u32[]{:S(2)}) %collective-permute-start.7) | collective-permute-done | bytes 589856 | tf_op jit(solution)/shard_map/ppermute | solution.py:262
  41.6 2.7 %final.2 = (bf16[192,4096]{1,0:T(8,128)(2,1)}, bf16[192,4096]{1,0:T(8,128)(2,1)}, bf16[192,4096]{1,0:T(8,128)(2,1)}, bf16[192,4096]{1,0:T(8,128)(2,1)}) custom-call(bf16[192,4096]{1,0:T(8,128)(2,1)S(1)} %get-tuple-element.66.q_ref.refs_0_, bf16[192,4096]{1,0:T(8,128)(2,1)S(1)} %get-tuple-element.67.k_ref.refs_1_, ...), custom_call_target="tpu_custom_call" | custom-call | flops 1000000000 | bytes 1024 | tf_op jit(solution)/shard_map/final/pallas_call | solution.py:249
  44.3 0.0 collective-permute-done.6.refs_7_
  44.3 2.3 %final.3 = (bf16[192,4096]{1,0:T(8,128)(2,1)}, bf16[192,4096]{1,0:T(8,128)(2,1)}, bf16[192,4096]{1,0:T(8,128)(2,1)}, bf16[192,4096]{1,0:T(8,128)(2,1)}) custom-call(bf16[192,4096]{1,0:T(8,128)(2,1)S(1)} %get-tuple-element.66.q_ref.refs_0_, ...), custom_call_target="tpu_custom_call", output_to_operand_aliasing={{0}: (12, {}), {1}: (13, {}), {2}: (14, {}), {3}: (15, {})} | custom-call | flops 1000000000 | bytes 1024 | tf_op jit(solution)/shard_map/final/pallas_call | solution.py:249
Async XLA Ops:
  3.9 2.1 %collective-permute-start.3 = (bf16[18,128,128]{2,1,0:T(8,128)(2,1)S(1)}, bf16[18,128,128]{2,1,0:T(8,128)(2,1)S(1)}, u32[]{:S(2)}, u32[]{:S(2)}) collective-permute-start(bf16[18,128,128]{2,1,0:T(8,128)(2,1)S(1)} %get-tuple-element.63), channel_id=1, source_target_pairs={{0,1},{1,0},{2,3},{3,2},{4,5},{5,4},{6,7},{7,6},{8,9},{9,8},{10,11... | collective-permute-start | bytes 1769480 | tf_op jit(solution)/shard_map/ppermute | solution.py:262
  4.7 2.6 %collective-permute-start = (bf16[14,128,128]{2,1,0:T(8,128)(2,1)S(1)}, bf16[14,128,128]{2,1,0:T(8,128)(2,1)S(1)}, u32[]{:S(2)}, u32[]{:S(2)}) collective-permute-start(bf16[14,128,128]{2,1,0:T(8,128)(2,1)S(1)} %get-tuple-element.55), channel_id=1, source_target_pairs={{0,1},{1,0},{2,3},{3,2},{4,5},{5,4},{6,7},{7,6},{8,9},{9,8},{10,11... | collective-permute-start | bytes 1376264 | tf_op jit(solution)/shard_map/ppermute | solution.py:262
  6.1 19.1 %collective-permute-start.4 = (bf16[18,128,128]{2,1,0:T(8,128)(2,1)S(1)}, bf16[18,128,128]{2,1,0:T(8,128)(2,1)S(1)}, u32[]{:S(2)}, u32[]{:S(2)}) collective-permute-start(bf16[18,128,128]{2,1,0:T(8,128)(2,1)S(1)} %plus.6.base_ref), channel_id=1, source_target_pairs={{0,2},{2,4},{3,1},{4,6},{5,3},{6,8},{7,5},{8,10},{9,7},{10,12},{11... | collective-permute-start | bytes 1769480 | tf_op jit(solution)/shard_map/ppermute | solution.py:266
  7.5 16.2 %collective-permute-start.1 = (bf16[14,128,128]{2,1,0:T(8,128)(2,1)S(1)}, bf16[14,128,128]{2,1,0:T(8,128)(2,1)S(1)}, u32[]{:S(2)}, u32[]{:S(2)}) collective-permute-start(bf16[14,128,128]{2,1,0:T(8,128)(2,1)S(1)} %plus.4.base_ref), channel_id=1, source_target_pairs={{0,4},{2,6},{4,8},{5,1},{6,10},{7,3},{8,12},{9,5},{10,14},{11,7},{... | collective-permute-start | bytes 1376264 | tf_op jit(solution)/shard_map/ppermute | solution.py:266
  23.8 15.8 %collective-permute-start.2 = (bf16[14,128,128]{2,1,0:T(8,128)(2,1)S(1)}, bf16[14,128,128]{2,1,0:T(8,128)(2,1)S(1)}, u32[]{:S(2)}, u32[]{:S(2)}) collective-permute-start(bf16[14,128,128]{2,1,0:T(8,128)(2,1)S(1)} %plus.5), channel_id=1, source_target_pairs={{0,2},{2,4},{3,1},{4,6},{5,3},{6,8},{7,5},{8,10},{9,7},{10,12},{11... | collective-permute-start | bytes 1376264 | tf_op jit(solution)/shard_map/ppermute | solution.py:266
  25.2 14.0 %collective-permute-start.5 = (bf16[18,128,128]{2,1,0:T(8,128)(2,1)S(1)}, bf16[18,128,128]{2,1,0:T(8,128)(2,1)S(1)}, u32[]{:S(2)}, u32[]{:S(2)}) collective-permute-start(bf16[18,128,128]{2,1,0:T(8,128)(2,1)S(1)} %plus.7), channel_id=1, source_target_pairs={{0,4},{2,6},{4,8},{5,1},{6,10},{7,3},{8,12},{9,5},{10,14},{11,7},{... | collective-permute-start | bytes 1769480 | tf_op jit(solution)/shard_map/ppermute | solution.py:266
  39.5 2.1 %collective-permute-start.7 = (bf16[18,128,128]{2,1,0:T(8,128)(2,1)S(1)}, bf16[18,128,128]{2,1,0:T(8,128)(2,1)S(1)}, u32[]{:S(2)}, u32[]{:S(2)}) collective-permute-start(bf16[18,128,128]{2,1,0:T(8,128)(2,1)S(1)} %get-tuple-element.75), channel_id=1, source_target_pairs={{0,1},{1,0},{2,3},{3,2},{4,5},{5,4},{6,7},{7,6},{8,9},{9,8},{10,11... | collective-permute-start | bytes 1769480 | tf_op jit(solution)/shard_map/ppermute | solution.py:262
  39.8 4.5 %collective-permute-start.6 = (bf16[14,128,128]{2,1,0:T(8,128)(2,1)S(1)}, bf16[14,128,128]{2,1,0:T(8,128)(2,1)S(1)}, u32[]{:S(2)}, u32[]{:S(2)}) collective-permute-start(bf16[14,128,128]{2,1,0:T(8,128)(2,1)S(1)} %get-tuple-element.78), channel_id=1, source_target_pairs={{0,1},{1,0},{2,3},{3,2},{4,5},{5,4},{6,7},{7,6},{8,9},{9,8},{10,11... | collective-permute-start | bytes 1376264 | tf_op jit(solution)/shard_map/ppermute | solution.py:262

commit v4 on v3

--- a/solution.py
+++ b/solution.py
@@ -65,7 +65,7 @@
         at += size
 
 
-def open_kernel(dev_ref, doc_hbm, q_hbm, k_hbm, v_hbm, g_hbm, q_ref, k_ref, v_ref, g_ref, keep_ref, send_ref, flag_ref, rows_ref, reach_ref, allowed_ref, doc_ref, doc_sem, sems, *, docs, sizes, scale):
+def open_kernel(dev_ref, doc_hbm, q_hbm, k_hbm, v_hbm, g_hbm, q_ref, k_ref, v_ref, g_ref, keep_ref, send_ref, flag_ref, rows_ref, reach_ref, allowed_ref, turned_ref, doc_ref, doc_sem, sems, *, docs, sizes, scale):
     rows, width = q_ref.shape
     arrays = ((k_hbm, k_ref), (v_hbm, v_ref), (q_hbm, q_ref), (g_hbm, g_ref))
     rest = width // DH - sum(sizes)
@@ -107,6 +107,7 @@
     t = lax.broadcasted_iota(jnp.int32, (rows, rows), 0)
     s = lax.broadcasted_iota(jnp.int32, (rows, rows), 1)
     allowed_ref[...] = jnp.where((s <= t) & ((t < start) | (s >= start)), 1.0, 0.0).astype(BF16)
+    turned_ref[...] = jnp.where((t <= s) & ((s < start) | (t >= start)), 1.0, 0.0).astype(BF16)
 
     def ready(c):
         for cp in copies[c]:
@@ -120,7 +121,7 @@
     tails_of(q_ref, k_ref, v_ref, g_ref, flag_ref, rows_ref, keep_ref, send_ref, lo, (n,))
 
 
-def local_kernel(q_ref, k_ref, v_ref, g_ref, allowed_ref, o_ref, dq_ref, dk_ref, dv_ref, *, lo, n, scale, unroll):
+def local_kernel(q_ref, k_ref, v_ref, g_ref, allowed_ref, turned_ref, o_ref, dq_ref, dk_ref, dv_ref, *, lo, n, scale, unroll):
     def step(j, carry):
         for u in range(unroll):
             i = j * unroll + u
@@ -129,36 +130,43 @@
             q, k, v, g = q_ref[:, src], k_ref[:, src], v_ref[:, src], g_ref[:, src]
             probs = dot_nt(q, k).astype(BF16) * allowed_ref[...]
             dprobs = dot_nt(g, v).astype(BF16) * allowed_ref[...]
+            probs_t = dot_nt(k, q).astype(BF16) * turned_ref[...]
+            dprobs_t = dot_nt(v, g).astype(BF16) * turned_ref[...]
             o_ref[:, dst] = (scale * dot_nn(probs, v)).astype(BF16)
             dq_ref[:, dst] = (scale * dot_nn(dprobs, k)).astype(BF16)
-            dk_ref[:, dst] = (scale * dot_tt(dprobs, q)).astype(BF16)
-            dv_ref[:, dst] = (scale * dot_tt(probs, g)).astype(BF16)
+            dk_ref[:, dst] = (scale * dot_nn(dprobs_t, q)).astype(BF16)
+            dv_ref[:, dst] = (scale * dot_nn(probs_t, g)).astype(BF16)
         return carry
 
     lax.fori_loop(0, n // unroll, step, 0)
 
 
-def final_kernel(q_ref, k_ref, v_ref, g_ref, flag_ref, reach_ref, mine_ref, other_ref, parts, outs, bufs, sems, *, lo, sizes):
+def final_kernel(q_ref, k_ref, v_ref, g_ref, flag_ref, reach_ref, shares, outs, bufs, pair_ref, sems, *, chunks):
     even = jnp.broadcast_to(flag_ref[EVEN : EVEN + 1, :], (DH, DH)) > 0
+    pair_ref[...] = jnp.zeros_like(pair_ref)
     copies = []
     at = 0
-    for c, size in enumerate(sizes):
-        for i in range(at, at + size):
-            cols = pl.ds(i * DH, DH)
-            src = pl.ds((lo + i) * DH, DH)
-            q, k, v, g = q_ref[:, src], k_ref[:, src], v_ref[:, src], g_ref[:, src]
-            mine, other = mine_ref[i].astype(F32), other_ref[i].astype(F32)
-            state = jnp.where(even, mine, other).astype(BF16)
-            back = jnp.where(even, other, mine).astype(BF16)
-            terms = ((0, dot_nn(q, state)), (0, dot_nt(g, state)), (1, dot_nt(v, back)), (1, dot_nn(k, back)))
+    for c, (share, size) in enumerate(chunks):
+        mine_ref, other_ref, *parts = shares[share]
+        base = 0 if share == 0 else shares[0][0].shape[0]
+        for i in range(at, at + size, 2):
+            slot = 2 * ((i // 2) % 2)
+            for u in range(2):
+                mine, other = mine_ref[i + u - base].astype(F32), other_ref[i + u - base].astype(F32)
+                own = pl.ds(u * DH, DH)
+                pair_ref[slot, own, own] = jnp.where(even, mine, other).astype(BF16)
+                pair_ref[slot + 1, own, own] = jnp.where(even, other, mine).astype(BF16)
+            src = pl.ds(i * DH, 2 * DH)
+            state, back = pair_ref[slot], pair_ref[slot + 1]
+            terms = ((0, dot_nn(q_ref[:, src], state)), (0, dot_nt(g_ref[:, src], state)), (1, dot_nt(v_ref[:, src], back)), (1, dot_nn(k_ref[:, src], back)))
             for a, (side, term) in enumerate(terms):
-                bufs[a][:, cols] = (parts[a][:, cols].astype(F32) + reach_ref[side] * term).astype(BF16)
+                for u in range(2):
+                    inner = pl.ds((i + u - base) * DH, DH)
+                    piece = parts[a][:, inner].astype(F32) + reach_ref[side] * term[:, u * DH : (u + 1) * DH]
+                    bufs[a][:, pl.ds((i + u) * DH, DH)] = piece.astype(BF16)
+        cols = pl.ds(at * DH, size * DH)
         for a in range(4):
-            cp = pltpu.make_async_copy(
-                bufs[a].at[:, pl.ds(at * DH, size * DH)],
-                outs[a].at[:, pl.ds((lo + at) * DH, size * DH)],
-                sems.at[c, a],
-            )
+            cp = pltpu.make_async_copy(bufs[a].at[:, cols], outs[a].at[:, cols], sems.at[c, a])
             cp.start()
             copies.append(cp)
         at += size
@@ -219,10 +227,11 @@
         out = pl.pallas_call(
             functools.partial(open_kernel, docs=docs, sizes=sizes, scale=scale),
             in_specs=[smem] + [hbm] * 5,
-            out_specs=[vmem] * 10,
+            out_specs=[vmem] * 11,
             out_shape=[shaped(rows, width)] * 4
             + [shaped(n, DH, DH)] * 2
-            + [jax.ShapeDtypeStruct((8, DH), F32), shaped(2, rows, DH), jax.ShapeDtypeStruct((2, rows, DH), F32), shaped(rows, rows)],
+            + [jax.ShapeDtypeStruct((8, DH), F32), shaped(2, rows, DH), jax.ShapeDtypeStruct((2, rows, DH), F32)]
+            + [shaped(rows, rows)] * 2,
             scratch_shapes=[pltpu.SMEM((docs,), jnp.int32), pltpu.SemaphoreType.DMA, pltpu.SemaphoreType.DMA((len(sizes) + 1, 4))],
             compiler_params=params,
             cost_estimate=pl.CostEstimate(flops=1000, transcendentals=0, bytes_accessed=1024),
@@ -235,28 +244,29 @@
         return call(body, (*blocks, flags, edge_rows), [shaped(n, DH, DH)] * 2, "tails", 1000000000)
 
     def local(blocks, lo, n, flops):
-        body = functools.partial(local_kernel, lo=lo, n=n, scale=scale, unroll=2)
-        return call(body, (*blocks, allowed), [shaped(rows, n * DH)] * 4, "local", flops)
-
-    def final(lo, n, mine, other, parts, outs):
-        aliased = [] if outs is None else list(outs)
-        sizes = split(n, 4)
+        body = functools.partial(local_kernel, lo=lo, n=n, scale=scale, unroll=max(u for u in range(1, 7) if n % u == 0))
+        return call(body, (*blocks, *allowed), [shaped(rows, n * DH)] * 4, "local", flops)
+
+    def final(share_x, share_w):
+        def chunked(n):
+            return split(n - 2, 4) + (2,)
+
+        chunks = [(0, size) for size in chunked(share_x[0].shape[0])] + [(1, size) for size in chunked(share_w[0].shape[0])]
 
         def body(*refs):
-            ins, rest = refs[:12], refs[12 + len(aliased) :]
-            final_kernel(*ins[:8], ins[8:], rest[:4], rest[4:8], rest[8], lo=lo, sizes=sizes)
+            shares = (refs[6:12], refs[12:18])
+            final_kernel(*refs[:6], shares, refs[18:22], refs[22:26], *refs[26:], chunks=chunks)
 
         return pl.pallas_call(
             body,
-            in_specs=[vmem] * 12 + [hbm] * len(aliased),
+            in_specs=[vmem] * 18,
             out_specs=[hbm] * 4,
             out_shape=[shaped(rows, width)] * 4,
-            scratch_shapes=[pltpu.VMEM((rows, n * DH), BF16)] * 4 + [pltpu.SemaphoreType.DMA((len(sizes), 4))],
-            input_output_aliases={12 + i: i for i in range(len(aliased))},
+            scratch_shapes=[pltpu.VMEM((rows, width), BF16)] * 4 + [pltpu.VMEM((4, 2 * DH, 2 * DH), BF16), pltpu.SemaphoreType.DMA((len(chunks), 4))],
             compiler_params=params,
             cost_estimate=pl.CostEstimate(flops=1000000000, transcendentals=0, bytes_accessed=1024),
             name="final",
-        )(*blocks, flags, reach, mine, other, *parts, *aliased)
+        )(*blocks, flags, reach, *share_x, *share_w)
 
     def across(x):
         return lax.ppermute(x, "seq", [(i, i ^ 1) for i in range(devices)])
@@ -272,7 +282,7 @@
         return call(close_kernel, (flags, near, far, keep), [shaped(*near.shape)] * 2, "close", 10000000000)
 
     n_w = n_heads - N_X
-    blocks, keep_x, send_x, (flags, edge_rows, reach, allowed) = opened(N_X)
+    blocks, keep_x, send_x, (flags, edge_rows, reach, *allowed) = opened(N_X)
     keep_w, send_w = tails(N_X, n_w)
     total_x = plus(across(send_x), 0, keep_x)
     total_w = plus(across(send_w), 0, keep_w)
@@ -289,12 +299,11 @@
     part_x = local(later, 0, N_X, 10000000000)
     far_x, part_x = lax.optimization_barrier((far_x, part_x))
     mine_x, pass_x = close(near_x, far_x, keep_x)
-    other_x = across(pass_x)
-    outs = final(0, N_X, mine_x, other_x, part_x, None)
     near_w, _ = lax.optimization_barrier((near_w, pass_x))
     mine_w, pass_w = close(near_w, far_w, keep_w)
+    other_x = across(pass_x)
     other_w = across(pass_w)
-    outs = final(N_X, n_w, mine_w, other_w, part_w, outs)
+    outs = final((mine_x, other_x, *part_x), (mine_w, other_w, *part_w))
     return tuple(outs)
 
 

time: 47 us -> 46.8 us (level)
  Pallas kernels: 23 us -> 18.7 us
  waiting for transfers between devices: 16.4 us -> 20.6 us
    ppermute x4, waiting for transfers between devices: 14.5 us -> 18 us  [along(): lax.ppermute(x, 'seq', [(i, j) for i, j in pairs if 0 <= j < devices])]
    pallas_call x9, Pallas kernels: 14.8 us -> 11.2 us  [call(): pl.pallas_call(body, in_specs=[vmem] * len(ins), out_specs=[vmem] * len(o...]
    pallas_call x2 -> x1, Pallas kernels: 5.04 us -> 4.24 us  [final(): pl.pallas_call(body, in_specs=[vmem] * 18, out_specs=[hbm] * 4, out_shape...]
    ppermute x4, waiting for transfers between devices: 1.88 us -> 2.53 us  [across(): return lax.ppermute(x, 'seq', [(i, i ^ 1) for i in range(devices)])]
  transfers between devices with their start and end apart: 8 -> 8, of which waited for: 4 -> 4; matrix products, arithmetic and copies ran while one was open for 0% -> 0% of each run, Pallas kernels for 37% -> 24%
where the time goes in v4:
time: 46.8 us; the launch traced here: 46.5 us
  waiting for transfers between devices  20.6 us (44%)
  Pallas kernels  18.7 us (40%)
  starting transfers between devices  6.43 us (14%)
  between operations  0.76 us (2%)
    ppermute x4, waiting for transfers between devices, along(): lax.ppermute(x, 'seq', [(i, j) for i, j in pairs if 0 <= j < devices])  18 us
    pallas_call x9, Pallas kernels, call(): pl.pallas_call(body, in_specs=[vmem] * len(ins), out_specs=[vmem] * len(o...  11.2 us
    ppermute x4, starting transfers between devices, along(): lax.ppermute(x, 'seq', [(i, j) for i, j in pairs if 0 <= j < devices])  5.17 us
    pallas_call x1, Pallas kernels, final(): pl.pallas_call(body, in_specs=[vmem] * 18, out_specs=[hbm] * 4, out_shape...  4.24 us
    pallas_call x1, Pallas kernels, opened(): pl.pallas_call(functools.partial(open_kernel, docs=docs, sizes=sizes, sca...  3.22 us
    ppermute x4, waiting for transfers between devices, across(): return lax.ppermute(x, 'seq', [(i, i ^ 1) for i in range(devices)])  2.53 us
    ppermute x4, starting transfers between devices, across(): return lax.ppermute(x, 'seq', [(i, i ^ 1) for i in range(devices)])  1.26 us
  transfers between devices with their start and end apart: 8, of which 4 were waited for; matrix products, arithmetic and copies ran while one was open for 0% of the time, Pallas kernels for 24%

profile of v4, /device:TPU:1, one launch (start us, length us, event | category | flops | bytes accessed | tf_op | source)
XLA Modules:
  0.0 46.5 jit_solution(10962607342932625516)
XLA Ops:
  0.6 3.2 %opened.1 = (bf16[192,4096]{1,0:T(8,128)(2,1)S(1)}, bf16[192,4096]{1,0:T(8,128)(2,1)S(1)}, bf16[192,4096]{1,0:T(8,128)(2,1)S(1)}, bf16[192,4096]{1,0:T(8,128)(2,...) custom-call(s32[1]{0:T(128)} %bitcast.dev_ref, ...), custom_call_target="tpu_custom_call" | custom-call | flops 1000 | bytes 1024 | tf_op jit(solution)/shard_map/opened/pallas_call | solution.py:227
  3.9 0.1 collective-permute-start
  3.9 0.8 %tails.1 = (bf16[14,128,128]{2,1,0:T(8,128)(2,1)S(1)}, bf16[14,128,128]{2,1,0:T(8,128)(2,1)S(1)}) custom-call(bf16[192,4096]{1,0:T(8,128)(2,1)S(1)} %get-tuple-element.64.q_ref.refs_0_, bf16[192,4096]{1,0:T(8,128)(2,1)S(1)} %get-tuple-element.65.k_ref.refs_1_, bf16[192,4096]{1,0:T(8,128)(2,1)S(1)} %get-tuple-element.66.v_ref.refs_2_, ...), custom_call_target="tpu_custom_call" | custom-call | flops 1000000000 | bytes 1024 | tf_op jit(solution)/shard_map/tails/pallas_call | solution.py:215
  4.7 0.6 %collective-permute-start.2 = (bf16[14,128,128]{2,1,0:T(8,128)(2,1)S(1)}, bf16[14,128,128]{2,1,0:T(8,128)(2,1)S(1)}, u32[]{:S(2)}, u32[]{:S(2)}) collective-permute-start(bf16[14,128,128]{2,1,0:T(8,128)(2,1)S(1)} %get-tuple-element.54), channel_id=1, source_target_pairs={{0,1},{1,0},{2,3},{3,2},{4,5},{5,4},{6,7},{7,6},{8,9},{9,8},{10,11... | collective-permute-start | bytes 1376264 | tf_op jit(solution)/shard_map/ppermute | solution.py:272
  5.3 0.6 %collective-permute-done.base_ref = bf16[18,128,128]{2,1,0:T(8,128)(2,1)S(1)} collective-permute-done((bf16[18,128,128]{2,1,0:T(8,128)(2,1)S(1)}, bf16[18,128,128]{2,1,0:T(8,128)(2,1)S(1)}, u32[]{:S(2)}, u32[]{:S(2)}) %collective-permute-start) | collective-permute-done | bytes 589856 | tf_op jit(solution)/shard_map/ppermute | solution.py:272
  5.9 0.1 plus.4.base_ref
  6.1 1.3 %collective-permute-start.1 = (bf16[18,128,128]{2,1,0:T(8,128)(2,1)S(1)}, bf16[18,128,128]{2,1,0:T(8,128)(2,1)S(1)}, u32[]{:S(2)}, u32[]{:S(2)}) collective-permute-start(bf16[18,128,128]{2,1,0:T(8,128)(2,1)S(1)} %plus.4.base_ref), channel_id=1, source_target_pairs={{0,2},{2,4},{3,1},{4,6},{5,3},{6,8},{7,5},{8,10},{9,7},{10,12},{11... | collective-permute-start | bytes 1769480 | tf_op jit(solution)/shard_map/ppermute | solution.py:276
  7.4 0.0 collective-permute-done.2.base_ref
  7.4 0.1 plus.5.base_ref
  7.5 1.3 %collective-permute-start.3 = (bf16[14,128,128]{2,1,0:T(8,128)(2,1)S(1)}, bf16[14,128,128]{2,1,0:T(8,128)(2,1)S(1)}, u32[]{:S(2)}, u32[]{:S(2)}) collective-permute-start(bf16[14,128,128]{2,1,0:T(8,128)(2,1)S(1)} %plus.5.base_ref), channel_id=1, source_target_pairs={{0,4},{2,6},{4,8},{5,1},{6,10},{7,3},{8,12},{9,5},{10,14},{11,7},{... | collective-permute-start | bytes 1376264 | tf_op jit(solution)/shard_map/ppermute | solution.py:276
  8.8 4.6 %local.2 = (bf16[192,1792]{1,0:T(8,128)(2,1)S(1)}, bf16[192,1792]{1,0:T(8,128)(2,1)S(1)}, bf16[192,1792]{1,0:T(8,128)(2,1)S(1)}, bf16[192,1792]{1,0:T(8,128)(2,1)S(1)}) custom-call(bf16[192,4096]{1,0:T(8,128)(2,1)S(1)} %get-tuple-element.64.q_ref.refs_0_, bf16[192,4096]{1,0:T(8,128)(2,1)S(1)} %get-tuple-element.65.k_ref.refs_1_, ...), custom_call_target="tpu_custom_call" | custom-call | flops 1000000000 | bytes 1024 | tf_op jit(solution)/shard_map/local/pallas_call | solution.py:215
  13.4 10.3 %collective-permute-done.3.x_ref.far_ref = bf16[14,128,128]{2,1,0:T(8,128)(2,1)S(1)} collective-permute-done((bf16[14,128,128]{2,1,0:T(8,128)(2,1)S(1)}, bf16[14,128,128]{2,1,0:T(8,128)(2,1)S(1)}, u32[]{:S(2)}, u32[]{:S(2)}) %collective-permute-start.3) | collective-permute-done | bytes 458784 | tf_op jit(solution)/shard_map/ppermute | solution.py:276
  23.7 0.1 plus.6
  23.8 1.3 %collective-permute-start.6 = (bf16[14,128,128]{2,1,0:T(8,128)(2,1)S(1)}, bf16[14,128,128]{2,1,0:T(8,128)(2,1)S(1)}, u32[]{:S(2)}, u32[]{:S(2)}) collective-permute-start(bf16[14,128,128]{2,1,0:T(8,128)(2,1)S(1)} %plus.6), channel_id=1, source_target_pairs={{0,2},{2,4},{3,1},{4,6},{5,3},{6,8},{7,5},{8,10},{9,7},{10,12},{11... | collective-permute-start | bytes 1376264 | tf_op jit(solution)/shard_map/ppermute | solution.py:276
  25.1 0.0 collective-permute-done.1.x_ref.near_ref
  25.1 0.1 plus.7
  25.3 1.3 %collective-permute-start.4 = (bf16[18,128,128]{2,1,0:T(8,128)(2,1)S(1)}, bf16[18,128,128]{2,1,0:T(8,128)(2,1)S(1)}, u32[]{:S(2)}, u32[]{:S(2)}) collective-permute-start(bf16[18,128,128]{2,1,0:T(8,128)(2,1)S(1)} %plus.7), channel_id=1, source_target_pairs={{0,4},{2,6},{4,8},{5,1},{6,10},{7,3},{8,12},{9,5},{10,14},{11,7},{... | collective-permute-start | bytes 1769480 | tf_op jit(solution)/shard_map/ppermute | solution.py:276
  26.6 5.0 %local.3 = (bf16[192,2304]{1,0:T(8,128)(2,1)S(1)}, bf16[192,2304]{1,0:T(8,128)(2,1)S(1)}, bf16[192,2304]{1,0:T(8,128)(2,1)S(1)}, bf16[192,2304]{1,0:T(8,128)(2,1)S(1)}) custom-call(bf16[192,4096]{1,0:T(8,128)(2,1)S(1)} %get-tuple-element.64.q_ref.refs_0_, bf16[192,4096]{1,0:T(8,128)(2,1)S(1)} %get-tuple-element.65.k_ref.refs_1_, ...), custom_call_target="tpu_custom_call" | custom-call | flops 10000000000 | bytes 1024 | tf_op jit(solution)/shard_map/local/pallas_call | solution.py:215
  31.5 7.7 %collective-permute-done.4.far_ref = bf16[18,128,128]{2,1,0:T(8,128)(2,1)S(1)} collective-permute-done((bf16[18,128,128]{2,1,0:T(8,128)(2,1)S(1)}, bf16[18,128,128]{2,1,0:T(8,128)(2,1)S(1)}, u32[]{:S(2)}, u32[]{:S(2)}) %collective-permute-start.4) | collective-permute-done | bytes 589856 | tf_op jit(solution)/shard_map/ppermute | solution.py:276
  39.2 0.2 close.2
  39.5 0.1 collective-permute-start.5
  39.6 0.0 collective-permute-done.6.near_ref
  39.6 0.2 close.3
  39.8 0.6 %collective-permute-start.7 = (bf16[14,128,128]{2,1,0:T(8,128)(2,1)S(1)}, bf16[14,128,128]{2,1,0:T(8,128)(2,1)S(1)}, u32[]{:S(2)}, u32[]{:S(2)}) collective-permute-start(bf16[14,128,128]{2,1,0:T(8,128)(2,1)S(1)} %get-tuple-element.81), channel_id=1, source_target_pairs={{0,1},{1,0},{2,3},{3,2},{4,5},{5,4},{6,7},{7,6},{8,9},{9,8},{10,11... | collective-permute-start | bytes 1376264 | tf_op jit(solution)/shard_map/ppermute | solution.py:272
  40.3 1.9 %collective-permute-done.7.refs_13_ = bf16[14,128,128]{2,1,0:T(8,128)(2,1)S(1)} collective-permute-done((bf16[14,128,128]{2,1,0:T(8,128)(2,1)S(1)}, bf16[14,128,128]{2,1,0:T(8,128)(2,1)S(1)}, u32[]{:S(2)}, u32[]{:S(2)}) %collective-permute-start.7) | collective-permute-done | bytes 458784 | tf_op jit(solution)/shard_map/ppermute | solution.py:272
  42.2 0.0 collective-permute-done.5.refs_7_
  42.2 4.2 %final.1 = (bf16[192,4096]{1,0:T(8,128)(2,1)}, bf16[192,4096]{1,0:T(8,128)(2,1)}, bf16[192,4096]{1,0:T(8,128)(2,1)}, bf16[192,4096]{1,0:T(8,128)(2,1)}) custom-call(bf16[192,4096]{1,0:T(8,128)(2,1)S(1)} %get-tuple-element.64.q_ref.refs_0_, bf16[192,4096]{1,0:T(8,128)(2,1)S(1)} %get-tuple-element.65.k_ref.refs_1_, ...), custom_call_target="tpu_custom_call" | custom-call | flops 1000000000 | bytes 1024 | tf_op jit(solution)/shard_map/final/pallas_call | solution.py:260
Async XLA Ops:
  3.9 2.1 %collective-permute-start = (bf16[18,128,128]{2,1,0:T(8,128)(2,1)S(1)}, bf16[18,128,128]{2,1,0:T(8,128)(2,1)S(1)}, u32[]{:S(2)}, u32[]{:S(2)}) collective-permute-start(bf16[18,128,128]{2,1,0:T(8,128)(2,1)S(1)} %get-tuple-element.51), channel_id=1, source_target_pairs={{0,1},{1,0},{2,3},{3,2},{4,5},{5,4},{6,7},{7,6},{8,9},{9,8},{10,11... | collective-permute-start | bytes 1769480 | tf_op jit(solution)/shard_map/ppermute | solution.py:272
  4.7 2.6 %collective-permute-start.2 = (bf16[14,128,128]{2,1,0:T(8,128)(2,1)S(1)}, bf16[14,128,128]{2,1,0:T(8,128)(2,1)S(1)}, u32[]{:S(2)}, u32[]{:S(2)}) collective-permute-start(bf16[14,128,128]{2,1,0:T(8,128)(2,1)S(1)} %get-tuple-element.54), channel_id=1, source_target_pairs={{0,1},{1,0},{2,3},{3,2},{4,5},{5,4},{6,7},{7,6},{8,9},{9,8},{10,11... | collective-permute-start | bytes 1376264 | tf_op jit(solution)/shard_map/ppermute | solution.py:272
  6.1 19.1 %collective-permute-start.1 = (bf16[18,128,128]{2,1,0:T(8,128)(2,1)S(1)}, bf16[18,128,128]{2,1,0:T(8,128)(2,1)S(1)}, u32[]{:S(2)}, u32[]{:S(2)}) collective-permute-start(bf16[18,128,128]{2,1,0:T(8,128)(2,1)S(1)} %plus.4.base_ref), channel_id=1, source_target_pairs={{0,2},{2,4},{3,1},{4,6},{5,3},{6,8},{7,5},{8,10},{9,7},{10,12},{11... | collective-permute-start | bytes 1769480 | tf_op jit(solution)/shard_map/ppermute | solution.py:276
  7.5 16.2 %collective-permute-start.3 = (bf16[14,128,128]{2,1,0:T(8,128)(2,1)S(1)}, bf16[14,128,128]{2,1,0:T(8,128)(2,1)S(1)}, u32[]{:S(2)}, u32[]{:S(2)}) collective-permute-start(bf16[14,128,128]{2,1,0:T(8,128)(2,1)S(1)} %plus.5.base_ref), channel_id=1, source_target_pairs={{0,4},{2,6},{4,8},{5,1},{6,10},{7,3},{8,12},{9,5},{10,14},{11,7},{... | collective-permute-start | bytes 1376264 | tf_op jit(solution)/shard_map/ppermute | solution.py:276
  23.8 15.8 %collective-permute-start.6 = (bf16[14,128,128]{2,1,0:T(8,128)(2,1)S(1)}, bf16[14,128,128]{2,1,0:T(8,128)(2,1)S(1)}, u32[]{:S(2)}, u32[]{:S(2)}) collective-permute-start(bf16[14,128,128]{2,1,0:T(8,128)(2,1)S(1)} %plus.6), channel_id=1, source_target_pairs={{0,2},{2,4},{3,1},{4,6},{5,3},{6,8},{7,5},{8,10},{9,7},{10,12},{11... | collective-permute-start | bytes 1376264 | tf_op jit(solution)/shard_map/ppermute | solution.py:276
  25.3 14.0 %collective-permute-start.4 = (bf16[18,128,128]{2,1,0:T(8,128)(2,1)S(1)}, bf16[18,128,128]{2,1,0:T(8,128)(2,1)S(1)}, u32[]{:S(2)}, u32[]{:S(2)}) collective-permute-start(bf16[18,128,128]{2,1,0:T(8,128)(2,1)S(1)} %plus.7), channel_id=1, source_target_pairs={{0,4},{2,6},{4,8},{5,1},{6,10},{7,3},{8,12},{9,5},{10,14},{11,7},{... | collective-permute-start | bytes 1769480 | tf_op jit(solution)/shard_map/ppermute | solution.py:276
  39.5 2.7 %collective-permute-start.5 = (bf16[18,128,128]{2,1,0:T(8,128)(2,1)S(1)}, bf16[18,128,128]{2,1,0:T(8,128)(2,1)S(1)}, u32[]{:S(2)}, u32[]{:S(2)}) collective-permute-start(bf16[18,128,128]{2,1,0:T(8,128)(2,1)S(1)} %get-tuple-element.74), channel_id=1, source_target_pairs={{0,1},{1,0},{2,3},{3,2},{4,5},{5,4},{6,7},{7,6},{8,9},{9,8},{10,11... | collective-permute-start | bytes 1769480 | tf_op jit(solution)/shard_map/ppermute | solution.py:272
  39.8 2.4 %collective-permute-start.7 = (bf16[14,128,128]{2,1,0:T(8,128)(2,1)S(1)}, bf16[14,128,128]{2,1,0:T(8,128)(2,1)S(1)}, u32[]{:S(2)}, u32[]{:S(2)}) collective-permute-start(bf16[14,128,128]{2,1,0:T(8,128)(2,1)S(1)} %get-tuple-element.81), channel_id=1, source_target_pairs={{0,1},{1,0},{2,3},{3,2},{4,5},{5,4},{6,7},{7,6},{8,9},{9,8},{10,11... | collective-permute-start | bytes 1376264 | tf_op jit(solution)/shard_map/ppermute | solution.py:272
